TPU v7x, 32 devices: a whole 2x2x4 slice. The times are simulated.
32 devices in a mesh: dp: 16 (over z, y, x), mp: 2 (over core).
Axes of the slice: x: 2, y: 2, z: 4, core: 2. Of those that a mesh axis runs over, the one named last changes fastest.
Arguments:
- tokens: bfloat16 [2, 512, 16, 768], P('mp', 'dp'), may hold values from -6 to 6
- cotangent: bfloat16 [2, 512, 16, 768], P('mp', 'dp'), may hold values from -6 to 6
- lengths: int32 [16], replicated, may hold values from 128 to 1024, as said below
- deal_order: int32 [16], replicated, may hold values from 0 to 15, as said below
- attn_in: bfloat16 [1, 3, 768, 768], P(None, None, 'dp', 'mp'), may hold values from -0.21875 to 0.21875
- attn_out: bfloat16 [1, 768, 768], P(None, 'mp', 'dp'), may hold values from -0.875 to 0.875
- ffn_in: bfloat16 [1, 768, 3072], P(None, 'dp', 'mp'), may hold values from -0.21875 to 0.21875
- ffn_out: bfloat16 [1, 3072, 768], P(None, 'mp', 'dp'), may hold values from -0.109375 to 0.109375
- attn_bias: bfloat16 [1, 2, 768], replicated, may hold values from -3 to 3
- ffn_bias: bfloat16 [1, 3072], replicated, may hold values from -3 to 3
- norm_gain: bfloat16 [1, 2, 768], replicated, may hold values from 0.5 to 1.5
- shifts: bfloat16 [1, 4, 768], replicated, may hold values from -3 to 3
Outputs:
- output: bfloat16 [2, 512, 16, 768], P('mp', 'dp')
- input_grad: bfloat16 [2, 512, 16, 768], P('mp', 'dp')
- attn_in_grad: float32 [1, 3, 768, 768], P(None, None, 'dp', 'mp')
- attn_out_grad: float32 [1, 768, 768], P(None, 'mp', 'dp')
- ffn_in_grad: float32 [1, 768, 3072], P(None, 'dp', 'mp')
- ffn_out_grad: float32 [1, 3072, 768], P(None, 'mp', 'dp')
- attn_bias_grad: float32 [1, 2, 768], replicated
- ffn_bias_grad: float32 [1, 3072], replicated
- norm_gain_grad: float32 [1, 2, 768], replicated
- shifts_grad: float32 [1, 4, 768], replicated
Inputs may be any that keep to these rules, and one draw needn't show every extreme that they name: `lengths`: some sequence has exactly 1024 valid tokens. `deal_order`: a permutation of the sequences; slot s is processed by data group s.
All inputs are finite; a program needn't handle non-finite values.
Results may differ from a plain program's by a relative error of at most 0.02.
Values may be sent and summed in bfloat16 or wider, within the bound.
No kernel may reach another device: no remote copies, remote signals or barrier semaphores. Data moves between devices by JAX's collectives and lax.ppermute only.
A program may use at most 128 MiB of HBM per device.

v0:
```python
import functools

import jax
import jax.numpy as jnp
from jax import lax
from jax.experimental import pallas as pl
from jax.experimental.pallas import tpu as pltpu
from jax.sharding import PartitionSpec as P

HEAD_DIM = 64
PAIR = 2 * HEAD_DIM

eps_norm = 1e-12
root_half = 0.7071067811865476
inv_root_two_pi = 0.3989422804014327
negative_fill = -1000000000.0
F32 = jnp.float32
BF16 = jnp.bfloat16


def matmul(a, b):
    return lax.dot_general(a, b, (((1,), (0,)), ((), ())), preferred_element_type=F32)


def matmul_nt(a, b):
    return lax.dot_general(a, b, (((1,), (1,)), ((), ())), preferred_element_type=F32)


def gradient(x, y):
    blocks = lax.axis_size("dp")
    if x.shape[1] % (16 * blocks) == 0:
        return Product(x, y, blocks)
    return matmul_tn(x, y).astype(BF16)


def matmul_tn(a, b):
    return lax.dot_general(a, b, (((0,), (0,)), ((), ())), preferred_element_type=F32)


FLOPS_PER_US = 172500000


def cost(us):
    return pl.CostEstimate(flops=int(us * FLOPS_PER_US), transcendentals=0, bytes_accessed=1000)


def xor_permute(x, axis, mask):
    n = lax.axis_size(axis)
    return lax.ppermute(x, axis, [(i, i ^ mask) for i in range(n)])


def dp_axes(n):
    bits = n.bit_length() - 1
    out, at = [], 0
    while at < bits:
        width = 1 if at < 2 else min(2, bits - at)
        out.append((at, 1 << width))
        at += width
    return out[::-1]


def stage_parts(x, shift, size):
    return [x] + [xor_permute(x, "dp", j << shift) for j in range(1, size)]


def stage_gather(x, axis, shift, size):
    return jnp.concatenate(stage_parts(x, shift, size), axis=0)


def assemble_kernel(count, orders, cuts, *refs):
    me = lax.axis_index("dp")
    sources = [(refs[2 * i], refs[2 * i + 1]) for i in range(len(orders))]
    targets = refs[2 * len(orders) :]

    @pl.loop(0, count)
    def _(block):
        place = lax.bitwise_xor(me, block)
        at = 0
        for (own, received), order in zip(sources, orders):
            spot, stride = 0, 1
            for shift, size in order[:-1]:
                spot = spot + stride * lax.bitwise_and(lax.shift_right_logical(place, shift), size - 1)
                stride *= size
            side = lax.bitwise_and(lax.shift_right_logical(place, order[-1][0]), 1)
            cols = own.shape[2]

            def write(source, at=at, cols=cols, spot=spot):
                start = 0
                for target, (low, high) in zip(targets, cuts):
                    first, last = max(low, at), min(high, at + cols)
                    if first < last:
                        target[block, :, first - low : last - low] = source[spot, :, first - at : last - at]

            @pl.when(side == 0)
            def _():
                write(own)

            @pl.when(side == 1)
            def _():
                write(received)

            at += cols


def tie(x, *others):
    return lax.optimization_barrier((x,) + others)[0]


def gather_first(x, order, name):
    with jax.named_scope(name + "_first"):
        y = x[None]
        for shift, size in order[:-2]:
            y = stage_gather(y, "dp", shift, size)
        return y


def gather_next(y, order, name):
    with jax.named_scope(name + "_next"):
        return stage_gather(y, "dp", *order[-2])


def gather_last(y, order, name):
    with jax.named_scope(name + "_last"):
        return [y, xor_permute(y, "dp", 1 << order[-1][0])]


def assemble(sides, orders, widths):
    count = lax.axis_size("dp")
    rows = sides[0].shape[1]
    cuts, at = [], 0
    for w in widths:
        cuts.append((at, at + w))
        at += w
    vmem = pl.BlockSpec(memory_space=pltpu.VMEM)
    outs = pl.pallas_call(
        functools.partial(assemble_kernel, count, tuple(tuple(o) for o in orders), tuple(cuts)),
        out_shape=tuple(jax.ShapeDtypeStruct((count, rows, w), sides[0].dtype) for w in widths),
        in_specs=[vmem] * len(sides),
        out_specs=(vmem,) * len(widths),
        compiler_params=pltpu.CompilerParams(vmem_limit_bytes=6 << 20),
        cost_estimate=cost(1.0),
        name="assemble",
    )(*sides)
    return [o.reshape(count * rows, -1) for o in outs]


class Product:
    def __init__(self, x, y, blocks):
        self.x, self.y = x, y
        self.shape = (blocks, x.shape[1] // blocks, y.shape[1])
        self.size = x.shape[1] * y.shape[1]


def route_kernel(plan, kinds, count_out, *refs):
    me = lax.axis_index("dp")
    ins, outs, refs = [], [], list(refs)
    for is_product in kinds:
        ins.append((refs.pop(0), refs.pop(0)) if is_product else refs.pop(0))
    outs, made = refs[:count_out], refs[count_out:]
    for index, is_product in enumerate(kinds):
        if is_product:
            x_ref, y_ref = ins[index]
            ins[index] = made.pop(0)
            ins[index][...] = matmul_tn(x_ref[...], y_ref[...]).astype(BF16).reshape(ins[index].shape)
    for pieces, sizes, at, shift, grouped in plan:
        size = sizes[at]
        inner = 1
        for extent in sizes[at + 1 :]:
            inner *= extent
        rest = inner
        for extent in sizes[:at]:
            rest *= extent
        coord = lax.bitwise_and(lax.shift_right_logical(me, shift), size - 1)
        log_inner = inner.bit_length() - 1
        if grouped:
            whole = outs.pop(0)
            targets = [whole.at[j * rest : (j + 1) * rest] for j in range(size)]
        else:
            targets = [outs.pop(0) for _ in range(size)]
        for j, target in enumerate(targets):
            side = j if grouped else lax.bitwise_xor(coord, j)

            @pl.loop(0, rest)
            def _(r, target=target, side=side):
                upper = lax.shift_right_logical(r, log_inner)
                source = (upper * size + side) * inner + lax.bitwise_and(r, inner - 1)
                col = 0
                for piece in pieces:
                    width = piece[0][2] - piece[0][1]
                    first, low, high = piece[0]
                    value = ins[first][source, :, low:high]
                    if len(piece) > 1:
                        value = value.astype(F32)
                        for index, low, high in piece[1:]:
                            value = value + ins[index][source, :, low:high].astype(F32)
                    target[r, :, col : col + width] = value.astype(BF16)
                    col += width


def route(groups, name, grouped=False):
    arrays, plan, shapes = [], [], []
    for pieces, left, axis in groups:
        entries = []
        for piece in pieces:
            entry = []
            for array, low, high in piece:
                known = [i for i, other in enumerate(arrays) if other is array]
                if not known:
                    known = [len(arrays)]
                    arrays.append(array)
                entry.append((known[0], low, high))
            entries.append(tuple(entry))
        at = left.index(axis)
        plan.append((tuple(entries), tuple(size for _, size in left), at, axis[0], grouped))
        total = sum(piece[0][2] - piece[0][1] for piece in pieces)
        array = pieces[0][0][0]
        if grouped:
            shapes.append((1, (array.shape[0], array.shape[1], total)))
        else:
            shapes.append((axis[1], (array.shape[0] // axis[1], array.shape[1], total)))
    vmem = pl.BlockSpec(memory_space=pltpu.VMEM)
    out_shape = [jax.ShapeDtypeStruct(shape, BF16) for size, shape in shapes for _ in range(size)]
    kinds = tuple(isinstance(array, Product) for array in arrays)
    operands, scratch = [], []
    for array, is_product in zip(arrays, kinds):
        operands += [array.x, array.y] if is_product else [array]
        if is_product:
            scratch.append(pltpu.VMEM(array.shape, BF16))
    flat = pl.pallas_call(
        functools.partial(route_kernel, tuple(plan), kinds, len(out_shape)),
        out_shape=out_shape,
        in_specs=[vmem] * len(operands),
        out_specs=[vmem] * len(out_shape),
        scratch_shapes=scratch,
        compiler_params=pltpu.CompilerParams(vmem_limit_bytes=(20 if scratch else 6) << 20),
        cost_estimate=cost(1.0),
        name=name,
    )(*operands)
    outs = []
    for size, _ in shapes:
        outs.append(list(flat[:size]))
        flat = flat[size:]
    return outs


class Scatter:
    def __init__(self, arrays, orders, axes, name, group_last=False):
        self.group_last = group_last
        n = lax.axis_size("dp")
        self.name = name
        self.orders = [list(o) for o in orders]
        self.lefts = [list(axes) for _ in orders]
        self.pieces = []
        shaped = {}
        for parts in arrays:
            pieces = []
            if parts is None:
                self.pieces.append(None)
                continue
            for g, low, high in parts:
                if id(g) not in shaped:
                    shaped[id(g)] = g if isinstance(g, Product) else g.reshape(n, g.shape[0] // n, g.shape[1])
                pieces.append([(shaped[id(g)], low, high)])
            self.pieces.append(pieces)
        self.count = 0

    def deal(self):
        self.count += 1
        merged = len(self.pieces) > 1 and len(self.lefts[0]) < 3 and self.lefts[0] == self.lefts[1]
        groups = []
        if merged:
            groups.append((sum(self.pieces, []), self.lefts[0], self.orders[0][0]))
            self.orders, self.lefts = self.orders[:1], self.lefts[:1]
        else:
            for parts, left, order in zip(self.pieces, self.lefts, self.orders):
                groups.append((parts, left, order[0]))
        self.grouped = self.group_last and len(groups) == 1 and len(self.lefts[0]) == 1
        self.dealt = route(groups, f"{self.name}_deal_{self.count}", self.grouped)
        return self.dealt

    def send(self):
        pieces, lefts, orders = [], [], []
        for parts, left, order in zip(self.dealt, self.lefts, self.orders):
            shift, size = order[0]
            with jax.named_scope(f"{self.name}_{self.count}"):
                if self.grouped:
                    n = lax.axis_size("dp")
                    members = [[i | (j << shift) for j in range(size)] for i in range(n) if not (i >> shift) % size]
                    whole = lax.all_to_all(
                        parts[0], "dp", split_axis=0, concat_axis=0, axis_index_groups=members, tiled=True
                    )
                    rest = whole.shape[0] // size
                    got = [whole[j * rest : (j + 1) * rest] for j in range(size)]
                else:
                    got = [parts[0]] + [
                        xor_permute(parts[j], "dp", j << shift) for j in range(1, size)
                    ]
            pieces.append([[(x, 0, x.shape[2]) for x in got]])
            lefts.append([axis for axis in left if axis != order[0]])
            orders.append(order[1:])
        self.pieces, self.lefts, self.orders = pieces, lefts, orders

    def set_part(self, i, parts):
        self.pieces[i] = Scatter([parts], [self.orders[i]], self.lefts[i], self.name).pieces[0]

    def deal_one(self, i):
        return route([(self.pieces[i], self.lefts[i], self.orders[i][0])], f"{self.name}_deal_1{i}")[0]

    def send_one(self, i, parts):
        self.count = 1
        shift, size = self.orders[i][0]
        with jax.named_scope(f"{self.name}_1{i}"):
            got = [parts[0]] + [xor_permute(parts[j], "dp", j << shift) for j in range(1, size)]
        self.pieces[i] = [[(x, 0, x.shape[2]) for x in got]]
        self.lefts[i] = [axis for axis in self.lefts[i] if axis != self.orders[i][0]]
        self.orders[i] = self.orders[i][1:]

    def after(self, *others):
        arrays = [x for (piece,) in self.pieces for x, _, _ in piece[1:]]
        arrays = list(lax.optimization_barrier((tuple(arrays), others))[0])
        self.pieces = [
            [[piece[0]] + [(arrays.pop(0), low, high) for _, low, high in piece[1:]]] for (piece,) in self.pieces
        ]

    def before(self, x):
        arrays = [y for (piece,) in self.pieces for y, _, _ in piece]
        x, arrays = lax.optimization_barrier((x, tuple(arrays)))
        arrays = list(arrays)
        self.pieces = [[[(arrays.pop(0), low, high) for _, low, high in piece]] for (piece,) in self.pieces]
        return x

    def total(self):
        outs = []
        for (piece,) in self.pieces:
            parts = [x[0].astype(F32) for x, _, _ in piece]
            while len(parts) > 1:
                parts = [parts[i] + parts[i + 1] for i in range(0, len(parts), 2)]
            outs.append(parts[0])
        return outs[0] if len(outs) == 1 else jnp.concatenate(outs, axis=1)

    def finish_stages(self):
        while self.orders[0]:
            self.deal()
            self.send()

    def finish(self):
        self.finish_stages()
        return self.total()


def attend_forward_kernel(block, qkv_ref, bias_ref, *refs):
    ctx_ref, lse_ref = refs[-2:]
    length = qkv_ref.shape[0]
    bias = bias_ref[...]
    for head in range(2):
        low = head * HEAD_DIM
        keys = qkv_ref[:, PAIR + low : PAIR + low + HEAD_DIM]
        values_t = qkv_ref[:, 2 * PAIR + low : 2 * PAIR + low + HEAD_DIM].T
        for start in range(0, length, block):
            queries = qkv_ref[start : start + block, low : low + HEAD_DIM]
            scores = matmul_nt(keys, queries) + bias
            top = jnp.max(scores, axis=0, keepdims=True)
            exponent = jnp.exp(scores - top)
            total = jnp.sum(exponent, axis=0, keepdims=True)
            context_t = matmul(values_t, exponent.astype(BF16)) * (1.0 / total)
            ctx_ref[start : start + block, low : low + HEAD_DIM] = context_t.T.astype(BF16)
            lse_ref[0, head : head + 1, start : start + block] = top + jnp.log(total)


def attend_forward(qkv, bias, first, pairs, total, known=()):
    length = qkv.shape[0]
    return pl.pallas_call(
        functools.partial(attend_forward_kernel, min(256, length)),
        grid=(pairs,),
        out_shape=(
            jax.ShapeDtypeStruct((length, total * PAIR), BF16),
            jax.ShapeDtypeStruct((total, 2, length), F32),
        ),
        in_specs=[
            pl.BlockSpec((length, 3 * PAIR), lambda p: (0, p + first)),
            pl.BlockSpec((length, 1), lambda p: (0, 0)),
        ]
        + [pl.BlockSpec(memory_space=pl.ANY)] * len(known),
        out_specs=(
            pl.BlockSpec((length, PAIR), lambda p: (0, p + first)),
            pl.BlockSpec((1, 2, length), lambda p: (p + first, 0, 0)),
        ),
        input_output_aliases={2: 0, 3: 1} if known else {},
        compiler_params=pltpu.CompilerParams(vmem_limit_bytes=10 << 20),
        cost_estimate=cost(5.9 * pairs),
        name="attend_forward",
    )(qkv, bias, *known)


def attend_backward_kernel(block, qkv_ref, dctx_ref, lse_ref, bias_ref, *refs):
    out_ref, sums_ref, dk_ref, dv_ref = refs[-4:]
    length = qkv_ref.shape[0]
    bias = bias_ref[...]
    for head in range(2):
        low = head * HEAD_DIM
        keys = qkv_ref[:, PAIR + low : PAIR + low + HEAD_DIM]
        keys_t = keys.T
        values = qkv_ref[:, 2 * PAIR + low : 2 * PAIR + low + HEAD_DIM]
        query_sum = jnp.zeros((1, HEAD_DIM), F32)
        for start in range(0, length, block):
            queries = qkv_ref[start : start + block, low : low + HEAD_DIM]
            grads = dctx_ref[start : start + block, low : low + HEAD_DIM]
            lse = lse_ref[0, head : head + 1, start : start + block]
            probs = jnp.exp(matmul_nt(keys, queries) + bias - lse)
            grad_probs = matmul_nt(values, grads)
            inner = jnp.sum(probs * grad_probs, axis=0, keepdims=True)
            grad_scores = (probs * (grad_probs - inner)).astype(BF16)
            dv = matmul(probs.astype(BF16), grads)
            dk = matmul(grad_scores, queries)
            if start == 0:
                dk_ref[...] = dk
                dv_ref[...] = dv
            else:
                dk_ref[...] += dk
                dv_ref[...] += dv
            dq = (matmul(keys_t, grad_scores) * HEAD_DIM ** (-0.5)).T
            query_sum = query_sum + jnp.sum(dq, axis=0, keepdims=True)
            out_ref[start : start + block, low : low + HEAD_DIM] = dq.astype(BF16)
        dk = dk_ref[...]
        dv = dv_ref[...]
        out_ref[:, PAIR + low : PAIR + low + HEAD_DIM] = dk.astype(BF16)
        out_ref[:, 2 * PAIR + low : 2 * PAIR + low + HEAD_DIM] = dv.astype(BF16)
        sums_ref[0, 0:1, low : low + HEAD_DIM] = query_sum
        sums_ref[0, 1:2, low : low + HEAD_DIM] = jnp.sum(dv, axis=0, keepdims=True)


def attend_backward(qkv, dctx, lse, bias, first, pairs, total, known=()):
    length = qkv.shape[0]
    return pl.pallas_call(
        functools.partial(attend_backward_kernel, min(256, length)),
        grid=(pairs,),
        out_shape=(
            jax.ShapeDtypeStruct((length, total * 3 * PAIR), BF16),
            jax.ShapeDtypeStruct((total, 2, PAIR), F32),
        ),
        in_specs=[
            pl.BlockSpec((length, 3 * PAIR), lambda p: (0, p + first)),
            pl.BlockSpec((length, PAIR), lambda p: (0, p + first)),
            pl.BlockSpec((1, 2, length), lambda p: (p + first, 0, 0)),
            pl.BlockSpec((length, 1), lambda p: (0, 0)),
        ]
        + [pl.BlockSpec(memory_space=pl.ANY)] * len(known),
        out_specs=(
            pl.BlockSpec((length, 3 * PAIR), lambda p: (0, p + first)),
            pl.BlockSpec((1, 2, PAIR), lambda p: (p + first, 0, 0)),
        ),
        input_output_aliases={4: 0, 5: 1} if known else {},
        scratch_shapes=[pltpu.VMEM((length, HEAD_DIM), F32), pltpu.VMEM((length, HEAD_DIM), F32)],
        compiler_params=pltpu.CompilerParams(vmem_limit_bytes=10 << 20),
        cost_estimate=cost(7.3 * pairs),
        name="attend_backward",
    )(qkv, dctx, lse, bias, *known)


def call(kernel, outs, args, name, us, vmem_mib=10, scratch=()):
    spec = pl.BlockSpec(memory_space=pltpu.VMEM)
    return pl.pallas_call(
        kernel,
        out_shape=[jax.ShapeDtypeStruct(shape, kind) for shape, kind in outs],
        in_specs=[spec] * len(args),
        out_specs=[spec] * len(outs),
        scratch_shapes=list(scratch),
        compiler_params=pltpu.CompilerParams(vmem_limit_bytes=vmem_mib << 20),
        cost_estimate=cost(us),
        name=name,
    )(*args)


def row_blocks(rows, block):
    block = min(block, rows)
    return rows // block, block


def rows_at(i, block):
    return pl.ds(pl.multiple_of(i * block, block), block)


def project_kernel(x_ref, w_ref, bias_ref, scale_ref, out_ref):
    count, block = row_blocks(x_ref.shape[0], 512)

    @pl.loop(0, count)
    def _(i):
        at = rows_at(i, block)
        out_ref[at, :] = ((matmul(x_ref[at, :], w_ref[...]) + bias_ref[...]) * scale_ref[...]).astype(BF16)


def part_kernel(low, high, x_ref, w_ref, out_ref):
    out_ref[...] = matmul_nt(x_ref[low:high, :], w_ref[...]).astype(BF16)


def exchanged_parts(x, w, name):
    half = x.shape[0] // 2
    own, got = [], []
    for number in range(2):
        (part,) = call(
            functools.partial(part_kernel, number * half, (number + 1) * half),
            [((half, w.shape[0]), BF16)],
            (x, w),
            f"{name}_{number}",
            1.5,
        )
        if number == 0:
            x = tie(x, part)
        own.append(part)
        with jax.named_scope(f"{name}_{number}"):
            got.append(xor_permute(part, "mp", 1))
    return own + got[::-1]


def halves(parts, body, rows, block):
    count, block = row_blocks(rows // 2, block)
    for number in range(2):
        own_ref, got_ref = parts[number], parts[2 + number]

        @pl.loop(0, count)
        def _(i, number=number, own_ref=own_ref, got_ref=got_ref):
            at = rows_at(i, block)
            total = own_ref[at, :].astype(F32) + got_ref[at, :].astype(F32)
            body(number, at, rows_at(i + number * count, block), total)


def middle_kernel(x_ref, p0, p1, p2, p3, vec_ref, w_ref, bias_ref, normed_ref, rstd_ref, low_ref, act_ref, slope_ref):
    def body(number, half_at, at, total):
        mixed = x_ref[at, :].astype(F32) + total + vec_ref[2:3, :]
        normed, rstd = norm_forward(mixed)
        normed_ref[at, :] = normed.astype(BF16)
        rstd_ref[at, :] = rstd
        low = (normed * vec_ref[0:1, :] + vec_ref[3:4, :]).astype(BF16)
        low_ref[at, :] = low
        u = matmul(low, w_ref[...]) + bias_ref[...]
        half_cdf = 0.5 * (1.0 + lax.erf(u * root_half))
        act_ref[at, :] = (u * half_cdf).astype(BF16)
        slope_ref[at, :] = (half_cdf + u * jnp.exp(-0.5 * u * u) * inv_root_two_pi).astype(BF16)

    halves((p0, p1, p2, p3), body, x_ref.shape[0], 256)


def outer_kernel(normed_ref, p0, p1, p2, p3, cot_own_ref, cot_got0, cot_got1, vec_ref, out_ref, low_ref, sums_ref, cot_ref):
    sums_ref[...] = jnp.zeros_like(sums_ref)

    half = cot_own_ref.shape[0]
    for index, source in enumerate((cot_own_ref, cot_got0, cot_got1)):
        low = 0 if index == 0 else half + (index - 1) * (half // 2)
        cot_ref[low : low + source.shape[0], :] = source[...]

    def body(number, half_at, at, total):
        mixed = normed_ref[at, :].astype(F32) * vec_ref[0:1, :] + vec_ref[3:4, :] + total + vec_ref[4:5, :]
        normed, rstd = norm_forward(mixed)
        if number == 0:
            out_ref[at, :] = (normed * vec_ref[1:2, :] + vec_ref[5:6, :]).astype(BF16)
        cot = cot_ref[at, :].astype(F32)
        grad, grad_gain, grad_shift = norm_backward(cot, normed, rstd, vec_ref[1:2, :])
        low_ref[at, :] = grad.astype(BF16)
        sums_ref[0:1, :] += grad_gain
        sums_ref[1:2, :] += grad_shift
        sums_ref[2:3, :] += jnp.sum(grad, axis=0, keepdims=True)

    halves((p0, p1, p2, p3), body, normed_ref.shape[0], 256)


def hidden_grad_kernel(grad_ref, w_ref, slope_ref, out_ref, sums_ref):
    count, block = row_blocks(grad_ref.shape[0], 256)
    sums_ref[...] = jnp.zeros_like(sums_ref)

    @pl.loop(0, count)
    def _(i):
        at = rows_at(i, block)
        grad = matmul(grad_ref[at, :], w_ref[...]) * slope_ref[at, :].astype(F32)
        out_ref[at, :] = grad.astype(BF16)
        sums_ref[...] += jnp.sum(grad, axis=0, keepdims=True)


def inner_kernel(
    grad_in_ref, p0, p1, p2, p3, normed_ref, rstd_ref, vec_ref, w_ref, own_grad_ref, low_ref, ctx_ref, sums_ref
):
    sums_ref[...] = jnp.zeros_like(sums_ref)

    def body(number, half_at, at, total):
        given = grad_in_ref[at, :].astype(F32) + total
        grad, grad_gain, grad_shift = norm_backward(given, normed_ref[at, :].astype(F32), rstd_ref[at, :], vec_ref[0:1, :])
        low = grad.astype(BF16)
        low_ref[at, :] = low
        ctx_ref[at, :] = matmul(low, w_ref[...]).astype(BF16)
        sums_ref[0:1, :] += grad_gain
        sums_ref[1:2, :] += grad_shift
        sums_ref[2:3, :] += jnp.sum(grad, axis=0, keepdims=True)
        if number == 0:
            own_grad_ref[at, :] = grad

    halves((p0, p1, p2, p3), body, normed_ref.shape[0], 256)


def input_grad_kernel(x_ref, w_ref, grad_ref, keep_ref, send_ref):
    half = keep_ref.shape[0]
    send_ref[...] = matmul_nt(x_ref[half:, :], w_ref[...]).astype(BF16)
    keep_ref[...] = grad_ref[...] + matmul_nt(x_ref[:half, :], w_ref[...])


def norm_forward(rows):
    center = rows - jnp.mean(rows, axis=1, keepdims=True)
    rstd = lax.rsqrt(jnp.mean(center * center, axis=1, keepdims=True) + eps_norm)
    return center * rstd, rstd


def norm_backward(grad, normed, rstd, gain):
    scaled = grad * gain
    inner = (
        scaled
        - jnp.mean(scaled, axis=1, keepdims=True)
        - normed * jnp.mean(scaled * normed, axis=1, keepdims=True)
    )
    return (
        rstd * inner,
        jnp.sum(grad * normed, axis=0, keepdims=True),
        jnp.sum(grad, axis=0, keepdims=True),
    )


def from_other(x):
    half = x.shape[0] // 2
    return [xor_permute(x[:half], "mp", 1), xor_permute(x[half:], "mp", 1)]


def deal_rows(x, deal_order):
    return x[0].at[:, deal_order].get(mode="promise_in_bounds").transpose(1, 0, 2)


def exchange_in(dealt, *others):
    dealt = tie(dealt, *others)
    arrived = lax.all_to_all(dealt, "dp", split_axis=0, concat_axis=0, tiled=True)
    return arrived.reshape(-1, dealt.shape[2])


def exchange_out(rows, extra):
    n = lax.axis_size("dp")
    with jax.named_scope("out_rows"):
        blocks = rows.reshape(n, rows.shape[0] // n, rows.shape[1])
        blocks = jnp.concatenate([blocks, jnp.broadcast_to(extra, (n,) + extra.shape)], axis=1)
        return lax.all_to_all(blocks, "dp", split_axis=0, concat_axis=0, tiled=True)


def taken_out(sent, count):
    return sent[:, :count].transpose(1, 0, 2)[None], sent[:, count:]


def put_split(out_ref, row, count, value):
    high = value.astype(BF16)
    out_ref[row : row + 1, :] = high
    out_ref[row + count : row + count + 1, :] = (value - high.astype(F32)).astype(BF16)


def early_kernel(one_ref, two_ref, up_ref, out_ref):
    first = lax.axis_index("mp") == 0
    width = one_ref.shape[1]
    pieces = up_ref.shape[1] // width
    count = 3 + pieces
    out_ref[...] = jnp.zeros_like(out_ref)
    for row in range(3):
        put_split(out_ref, row, count, jnp.where(first, one_ref[row : row + 1, :], two_ref[row : row + 1, :]))
    for piece in range(pieces):
        put_split(out_ref, 3 + piece, count, up_ref[0:1, piece * width : (piece + 1) * width])


def late_kernel(pairs, keep_ref, g0, g1, sums_ref, rows_ref, out_ref):
    half = keep_ref.shape[0] // 2
    for index, source in enumerate((g0, g1)):
        at = slice(index * half, (index + 1) * half)
        rows_ref[at, :] = (keep_ref[at, :] + source[...].astype(F32)).astype(BF16)
    out_ref[...] = jnp.zeros_like(out_ref)
    for which in range(2):
        for pair in range(pairs):
            col = (which * pairs + pair) * PAIR
            value = sums_ref[pair, which : which + 1, :]
            high = value.astype(BF16)
            out_ref[0:1, col : col + PAIR] = high
            out_ref[1:2, col : col + PAIR] = (value - high.astype(F32)).astype(BF16)


def gathered_kernel(count, x_ref, out_ref):
    out_ref[...] = jnp.zeros_like(out_ref)

    @pl.loop(0, x_ref.shape[0])
    def _(i):
        x = x_ref[i].astype(F32)
        out_ref[...] += x[:count, :] + x[count : 2 * count, :]


def local(
    tokens, cotangent, lengths, deal_order, attn_in, attn_out, ffn_in, ffn_out,
    attn_bias, ffn_bias, norm_gain, shifts,
):
    dp_size = lax.axis_size("dp")
    mp_rank = lax.axis_index("mp")
    dp_rank = lax.axis_index("dp")
    axes = dp_axes(dp_size)
    low = axes[-2:]
    high = axes[:-2]
    order_one = high + low
    order_two = high + low[::-1]
    back_one = low[::-1] + high[::-1]
    back_two = low + high[::-1]

    width = tokens.shape[3]
    half_len = tokens.shape[1] * dp_size
    seq_len = 2 * half_len
    head_cols = attn_in.shape[3]
    hidden_cols = ffn_in.shape[2]
    pairs = head_cols // PAIR
    shard_rows = attn_in.shape[2]

    three = attn_in[0].reshape(3, shard_rows, pairs, PAIR).transpose(1, 2, 0, 3)
    three = three.reshape(shard_rows, 3 * head_cols)
    back_t = attn_out[0].T
    up = ffn_in[0]
    down_t = ffn_out[0].T

    cut_three = 128 * ((3 * head_cols // 128 + 1) // 2)
    pieces_three = [three[:, :cut_three], three[:, cut_three:]]
    rest = jnp.concatenate([back_t, up], axis=1)
    cut_rest = 128 * ((rest.shape[1] // 128 + 1) // 2)
    orders = [tuple(order_one), tuple(order_two)]

    first_three = gather_first(three, order_one, "ag_three")
    with jax.named_scope("in_tokens"):
        tok_own = exchange_in(deal_rows(tokens, deal_order), first_three)
        dealt_cot = deal_rows(cotangent, deal_order)
    w_down = lax.all_gather(down_t, "dp", axis=0, tiled=True)
    next_three = [
        gather_next(first_three[:, :, :cut_three], order_one, "ag_three"),
        gather_next(first_three[:, :, cut_three:], order_two, "ag_three"),
    ]
    rest, *next_three = lax.optimization_barrier((rest, *next_three))
    with jax.named_scope("ag_rest_first"):
        first_got = [rest[None]]
        for shift, size in order_one[:-3]:
            first_got = [stage_gather(x, "dp", shift, size) for x in first_got]
        shift, size = order_one[-3]
        first_own = first_got[0]
        first_got = [xor_permute(first_own, "dp", j << shift) for j in range(1, size)]
    sides_three = gather_last(next_three[0], order_one, "ag_three") + gather_last(
        next_three[1], order_two, "ag_three"
    )
    (w_three,) = assemble(sides_three, orders, [3 * head_cols])
    hb = jnp.concatenate([tok_own] + from_other(tok_own), axis=0)
    length = lengths[deal_order[dp_rank]]
    place = jnp.arange(seq_len, dtype=jnp.int32)
    place = jnp.where(mp_rank == 0, place, (place + half_len) % seq_len)
    bias_col = jnp.where(place < length, 0.0, negative_fill).astype(F32)[:, None]

    def own_cols(v, count):
        return jnp.where(mp_rank == 0, v[..., :count], v[..., count:])

    bias_pair = own_cols(attn_bias[0].astype(F32), head_cols).reshape(2, pairs, PAIR)
    bias_three = jnp.stack([bias_pair[0], jnp.zeros_like(bias_pair[0]), bias_pair[1]], axis=1).reshape(1, -1)
    bias_up = own_cols(ffn_bias[0].astype(F32), hidden_cols)[None]
    scale_three = jnp.concatenate(
        [jnp.full((pairs, 1, PAIR), HEAD_DIM ** (-0.5), F32), jnp.ones((pairs, 2, PAIR), F32)], axis=1
    ).reshape(1, -1)
    vec = jnp.concatenate([norm_gain[0], shifts[0]], axis=0).astype(F32)
    hb, bias_up, vec, bias_col, dealt_cot = lax.optimization_barrier((hb, bias_up, vec, bias_col, dealt_cot))
    big, wide, hidden_shape = (seq_len, width), (seq_len, head_cols), (seq_len, hidden_cols)

    (qkv,) = call(
        project_kernel, [((seq_len, 3 * head_cols), BF16)], (hb, w_three, bias_three, scale_three), "project", 2.4
    )
    attended = attend_forward(qkv, bias_col, 0, 1, pairs)
    attended, *first_got = lax.optimization_barrier((attended, *first_got))
    first_rest = jnp.concatenate([first_own] + first_got, axis=0)
    attended, first_rest = lax.optimization_barrier((attended, first_rest))
    own_rest = [first_rest[:, :, :cut_rest], first_rest[:, :, cut_rest:]]
    with jax.named_scope("ag_rest_next"):
        got_rest = [xor_permute(y, "dp", 1 << o[-2][0]) for y, o in zip(own_rest, orders)]
    if pairs > 2:
        attended = attend_forward(qkv, bias_col, 1, pairs - 2, pairs, attended)
    attended, *got_rest = lax.optimization_barrier((attended, *got_rest))
    next_rest = [jnp.concatenate(pair, axis=0) for pair in zip(own_rest, got_rest)]
    attended, *next_rest = lax.optimization_barrier((attended, *next_rest))
    sides_rest = gather_last(next_rest[0], order_one, "ag_rest") + gather_last(
        next_rest[1], order_two, "ag_rest"
    )
    if pairs > 1:
        attended = attend_forward(qkv, bias_col, pairs - 1, 1, pairs, attended)
    context, lse = attended
    with jax.named_scope("in_cot"):
        cot_own = exchange_in(dealt_cot, context)
    context, w_down = lax.optimization_barrier((context, w_down))
    w_back, w_up = assemble(sides_rest, orders, [head_cols, hidden_cols])
    mid_normed, mid_rstd, mid_low, hidden_low, slope = call(
        middle_kernel,
        [(big, BF16), ((seq_len, 1), F32), (big, BF16), (hidden_shape, BF16), (hidden_shape, BF16)],
        (hb, *exchanged_parts(context, w_back, "attn_part"), vec, w_up, bias_up),
        "middle",
        8,
    )

    result, grad_two_low, sums_two = call(
        outer_kernel,
        [((half_len, width), BF16), (big, BF16), ((3, width), F32)],
        (
            mid_normed,
            *exchanged_parts(hidden_low, w_down, "ffn_part"),
            cot_own,
            *from_other(cot_own),
            vec,
        ),
        "outer",
        4.5,
        scratch=[pltpu.VMEM(big, BF16)],
    )
    ffn = Scatter(
        [[(gradient(grad_two_low, hidden_low), 0, hidden_cols)], None], [back_one, back_two], axes, "rs_ffn", True
    )
    dealt = ffn.deal_one(0)
    grad_two_low, dealt = lax.optimization_barrier((grad_two_low, dealt))
    ffn.send_one(0, dealt)
    grad_hidden_low, grad_up_bias = call(
        hidden_grad_kernel,
        [(hidden_shape, BF16), ((1, hidden_cols), F32)],
        (grad_two_low, w_down, slope),
        "hidden_grad",
        3.3,
    )
    parts = exchanged_parts(grad_hidden_low, w_up, "mid_part")
    grad_hidden_low = tie(grad_hidden_low, parts[1])
    ffn.set_part(1, [(gradient(mid_low, grad_hidden_low), 0, hidden_cols)])
    dealt = ffn.deal_one(1)
    parts[2], dealt = lax.optimization_barrier((parts[2], dealt))
    ffn.send_one(1, dealt)
    grad_one, grad_one_low, grad_context, sums_one = call(
        inner_kernel,
        [((half_len, width), F32), (big, BF16), (wide, BF16), ((3, width), F32)],
        (grad_two_low, *parts, mid_normed, mid_rstd, vec, w_back),
        "inner",
        3.5,
    )
    early_count = 3 + hidden_cols // width
    (early,) = call(
        early_kernel, [((16 * -(-2 * early_count // 16), width), BF16)], (sums_one, sums_two, grad_up_bias), "early", 0.5
    )
    sent_tokens = exchange_out(result, early)
    grad_w_back = gradient(grad_one_low, context)

    given = ()
    if pairs > 1:
        given = attend_backward(qkv, grad_context, lse, bias_col, 0, pairs - 1, pairs)
        ffn.after(given)
    ffn.deal()
    grad_context, ffn.dealt = lax.optimization_barrier((grad_context, ffn.dealt))
    ffn.send()
    given = attend_backward(qkv, grad_context, lse, bias_col, pairs - 1, 1, pairs, given)
    dqkv, pair_sums = given
    ffn.after(given)
    ffn.deal()
    dqkv, ffn.dealt = lax.optimization_barrier((dqkv, ffn.dealt))
    ffn.send()
    grad_w_three = gradient(hb, dqkv)
    cut = 128 * ((4 * head_cols // 128 + 1) // 2)
    tail = Scatter(
        [
            [(grad_w_three, 0, cut)],
            [(grad_w_three, cut, 3 * head_cols), (grad_w_back, 0, head_cols)],
        ],
        [back_one, back_two],
        axes,
        "rs_attn",
    )
    tail.deal()
    dqkv, tail.dealt = lax.optimization_barrier((dqkv, tail.dealt))
    tail.send()
    keep, sent = call(
        input_grad_kernel,
        [((half_len, width), F32), ((half_len, width), BF16)],
        (dqkv, w_three, grad_one),
        "input_grad",
        2.3,
    )
    got = from_other(sent)
    got, sent_tokens = lax.optimization_barrier((got, sent_tokens))
    grad_in, late = call(
        functools.partial(late_kernel, pairs),
        [((half_len, width), BF16), ((8, 2 * head_cols), BF16)],
        (keep, *got, pair_sums),
        "late",
        1.0,
    )
    sent_grad = exchange_out(grad_in, late)
    block = half_len // dp_size
    out_tokens, early_all = taken_out(sent_tokens, block)
    out_grad, late_all = taken_out(sent_grad, block)
    ffn_sum = ffn.finish()
    down_sum, up_sum = ffn_sum[:, :hidden_cols], ffn_sum[:, hidden_cols:]
    attn_sum = tail.finish()
    three_sum, back_sum = attn_sum[:, : 3 * head_cols], attn_sum[:, 3 * head_cols :]

    (early_sum,) = call(
        functools.partial(gathered_kernel, early_count), [((early_count, width), F32)], (early_all,), "early_sum", 0.5
    )
    (late_sum,) = call(functools.partial(gathered_kernel, 1), [((1, width), F32)], (late_all,), "late_sum", 0.5)

    def in_order(own):
        other = xor_permute(own, "mp", 1)
        return jnp.where(mp_rank == 0, own, other), jnp.where(mp_rank == 0, other, own)

    low_early, high_early = in_order(early_sum)
    low_late, high_late = in_order(late_sum)
    gain_out = jnp.stack([low_early[0], high_early[0]])[None]
    shift_out = jnp.stack([low_early[2], low_early[1], high_early[2], high_early[1]])[None]
    ffn_bias_out = jnp.concatenate([low_early[3:].reshape(1, -1), high_early[3:].reshape(1, -1)], axis=1)
    attn_bias_out = jnp.concatenate(
        [low_late.reshape(1, 2, head_cols), high_late.reshape(1, 2, head_cols)], axis=2
    )

    three_out = three_sum.reshape(shard_rows, pairs, 3, PAIR)
    three_out = three_out.transpose(2, 0, 1, 3).reshape(1, 3, shard_rows, head_cols)
    back_out = back_sum.T[None]
    up_out = up_sum[None]
    down_out = down_sum.T[None]
    return (
        out_tokens, out_grad, three_out, back_out, up_out, down_out,
        attn_bias_out, ffn_bias_out, gain_out, shift_out,
    )


def solution(mesh):
    placed = (
        P("mp", "dp", None, None),
        P("mp", "dp", None, None),
        P(),
        P(),
        P(None, None, "dp", "mp"),
        P(None, "mp", "dp"),
        P(None, "dp", "mp"),
        P(None, "mp", "dp"),
        P(),
        P(),
        P(),
        P(),
    )
    return jax.shard_map(
        local,
        mesh=mesh,
        in_specs=placed,
        out_specs=(
            P("mp", "dp", None, None),
            P("mp", "dp", None, None),
            P(None, None, "dp", "mp"),
            P(None, "mp", "dp"),
            P(None, "dp", "mp"),
            P(None, "mp", "dp"),
            P(),
            P(),
            P(),
            P(),
        ),
        check_vma=False,
    )
```

profile of v0, /device:TPU:0, one launch (start us, length us, event | category | flops | bytes accessed | tf_op | source)
XLA Modules:
  0.0 302.9 jit_solution(17598466813549820241)
XLA Ops:
  8.5 5.1 %collective-permute-start.2 = (bf16[1,48,1152]{2,1,0:T(8,128)(2,1)S(1)}, bf16[1,48,1152]{2,1,0:T(8,128)(2,1)S(1)}, u32[]{:S(2)}, u32[]{:S(2)}) collective-permute-start(bf16[1,48,1152]{2,1,0:T(8,128)(2,1)S(1)} %broadcast_in_dim_reshape.3), channel_id=1, source_target_pairs={{0,24},{2,26},{4,28},{6,30},{8,16},{10,18},{12,20},{14,22},{16,8},... | collective-permute-start | bytes 331784 | tf_op jit(solution)/shard_map/ag_three_first/ppermute | solution.py:49
  22.9 5.8 %all-to-all-start = ((bf16[16,32,768]{2,1,0:T(8,128)(2,1)}), bf16[16,32,768]{2,1,0:T(8,128)(2,1)S(1)}, u32[]{:S(2)}, u32[]{:S(2)}) async-start(bf16[16,32,768]{2,1,0:T(8,128)(2,1)} %gather_fusion), calls=%async_computation | async-start | bytes 1572864 | tf_op jit(solution)/shard_map/in_tokens/all_to_all | solution.py:635
  40.1 3.9 %collective-permute-done.5 = bf16[4,48,640]{2,1,0:T(8,128)(2,1)S(1)} collective-permute-done((bf16[4,48,640]{2,1,0:T(8,128)(2,1)S(1)}, bf16[4,48,640]{2,1,0:T(8,128)(2,1)S(1)}, u32[]{:S(2)}, u32[]{:S(2)}) %collective-permute-start.5) | collective-permute-done | bytes 245792 | tf_op jit(solution)/shard_map/ag_three_next/ppermute | solution.py:49
  50.2 5.0 %collective-permute-start.11 = (bf16[1,48,1920]{2,1,0:T(8,128)(2,1)}, bf16[1,48,1920]{2,1,0:T(8,128)(2,1)S(1)}, u32[]{:S(2)}, u32[]{:S(2)}) collective-permute-start(bf16[1,48,1920]{2,1,0:T(8,128)(2,1)} %bitcast.87), channel_id=1, source_target_pairs={{0,24},{2,26},{4,28},{6,30},{8,16},{10,18},{12,20},{14,22},{16,8},... | collective-permute-start | bytes 552968 | tf_op jit(solution)/shard_map/ag_rest_first/ppermute | solution.py:49
  68.1 5.9 %attend_forward.3 = (bf16[1024,384]{1,0:T(8,128)(2,1)S(1)}, f32[3,2,1024]{2,1,0:T(2,128)S(1)}) custom-call(bf16[1024,1152]{1,0:T(8,128)(2,1)S(1)} %project.1.qkv_ref, f32[1024,1]{1,0:T(8,128)S(1)} %fusion.5.bias_ref), custom_call_target="tpu_custom_call" | custom-call | flops 1017750016 | bytes 1000 | tf_op jit(solution)/shard_map/attend_forward/pallas_call | solution.py:372
  78.0 5.9 %attend_forward.4 = (bf16[1024,384]{1,0:T(8,128)(2,1)S(1)}, f32[3,2,1024]{2,1,0:T(2,128)S(1)}) custom-call(bf16[1024,1152]{1,0:T(8,128)(2,1)S(1)} %project.1.qkv_ref, f32[1024,1]{1,0:T(8,128)S(1)} %fusion.5.bias_ref, bf16[1024,384]{1,0:T(8,128)(2,1)S(1)} %get-tuple-element.130.refs_0_, ...), custom_call_target="tpu_custom_call", output_to_operand_aliasing={{0}: (2, {}), {1}: (3, {})} | custom-call | flops 1017750016 | bytes 1000 | tf_op jit(solution)/shard_map/attend_forward/pallas_call | solution.py:372
  83.9 7.8 %collective-permute-done.13 = bf16[4,48,896]{2,1,0:T(8,128)(2,1)S(1)} collective-permute-done((bf16[4,48,896]{2,1,0:T(8,128)(2,1)S(1)}, bf16[4,48,896]{2,1,0:T(8,128)(2,1)S(1)}, u32[]{:S(2)}, u32[]{:S(2)}) %collective-permute-start.13) | collective-permute-done | bytes 344096 | tf_op jit(solution)/shard_map/ag_rest_next/ppermute | solution.py:49
  95.0 6.3 %attend_forward.5 = (bf16[1024,384]{1,0:T(8,128)(2,1)S(1)}, f32[3,2,1024]{2,1,0:T(2,128)S(1)}) custom-call(bf16[1024,1152]{1,0:T(8,128)(2,1)S(1)} %project.1.qkv_ref, f32[1024,1]{1,0:T(8,128)S(1)} %fusion.5.bias_ref, bf16[1024,384]{1,0:T(8,128)(2,1)S(1)} %get-tuple-element.139.refs_0_, ...), custom_call_target="tpu_custom_call", output_to_operand_aliasing={{0}: (2, {}), {1}: (3, {})} | custom-call | flops 1017750016 | bytes 1000 | tf_op jit(solution)/shard_map/attend_forward/pallas_call | solution.py:372
  101.3 5.7 %all-to-all-start.1 = ((bf16[16,32,768]{2,1,0:T(8,128)(2,1)}), bf16[16,32,768]{2,1,0:T(8,128)(2,1)}, u32[]{:S(2)}, u32[]{:S(2)}) async-start(bf16[16,32,768]{2,1,0:T(8,128)(2,1)} %gather_fusion.1), calls=%async_computation.1 | async-start | bytes 1572864 | tf_op jit(solution)/shard_map/in_cot/all_to_all | solution.py:635
  107.0 8.6 %collective-permute-done.15.refs_3_ = bf16[8,48,896]{2,1,0:T(8,128)(2,1)S(1)} collective-permute-done((bf16[8,48,896]{2,1,0:T(8,128)(2,1)S(1)}, bf16[8,48,896]{2,1,0:T(8,128)(2,1)S(1)}, u32[]{:S(2)}, u32[]{:S(2)}) %collective-permute-start.15) | collective-permute-done | bytes 688160 | tf_op jit(solution)/shard_map/ag_rest_last/ppermute | solution.py:49
  123.5 6.1 %middle.1 = (bf16[1024,768]{1,0:T(8,128)(2,1)S(1)}, f32[1024,1]{1,0:T(8,128)S(1)}, bf16[1024,768]{1,0:T(8,128)(2,1)S(1)}, bf16[1024,1536]{1,0:T(8,128)(2,1)S(1)}, bf16[1024,1536]{1,0:T(8,128)(2,1)S(1)}) custom-call(bf16[1024,768]{1,0:T(8,128)(2,1)S(1)} %copy-done.1, bf16[512,768]{1,0:T(8,128)(2,1)S(1)} %attn_part_0.1.p0, ...), custom_call_target="tpu_custom_call" | custom-call | flops 1380000000 | bytes 1000 | tf_op jit(solution)/shard_map/middle/pallas_call | solution.py:462
  140.1 5.5 %outer.1 = (bf16[512,768]{1,0:T(8,128)(2,1)S(1)}, bf16[1024,768]{1,0:T(8,128)(2,1)S(1)}, f32[3,768]{1,0:T(4,128)S(1)}) custom-call(bf16[1024,768]{1,0:T(8,128)(2,1)S(1)} %copy-done.15, bf16[512,768]{1,0:T(8,128)(2,1)} %ffn_part_0.1.p0, bf16[512,768]{1,0:T(8,128)(2,1)} %ffn_part_1.1.p1, bf16[512,768]{1,0:T(8,128)(2,1)} %collective-permute-done.18.p2, ...), custom_call_target="tpu_custom_call" | custom-call | flops 776249984 | bytes 1000 | tf_op jit(solution)/shard_map/outer/pallas_call | solution.py:462
  145.6 3.8 %rs_ffn_deal_10.1 = (bf16[8,48,1536]{2,1,0:T(8,128)(2,1)S(1)}, bf16[8,48,1536]{2,1,0:T(8,128)(2,1)}) custom-call(bf16[1024,768]{1,0:T(8,128)(2,1)S(1)} %get-tuple-element.159.refs_0_.grad_ref.grad_in_ref, bf16[1024,1536]{1,0:T(8,128)(2,1)S(1)} %get-tuple-element.153.x_ref.refs_1_), custom_call_target="tpu_custom_call" | custom-call | flops 172500000 | bytes 1000 | tf_op jit(solution)/shard_map/rs_ffn_deal_10/pallas_call | solution.py:229
  156.2 3.9 %rs_ffn_deal_11.1 = (bf16[8,48,1536]{2,1,0:T(8,128)(2,1)S(1)}, bf16[8,48,1536]{2,1,0:T(8,128)(2,1)}) custom-call(bf16[1024,768]{1,0:T(8,128)(2,1)S(1)} %copy-done.25, bf16[1024,1536]{1,0:T(8,128)(2,1)S(1)} %get-tuple-element.164.x_ref.refs_1_), custom_call_target="tpu_custom_call" | custom-call | flops 172500000 | bytes 1000 | tf_op jit(solution)/shard_map/rs_ffn_deal_11/pallas_call | solution.py:229
  168.4 9.1 %all-to-all-start.2 = ((bf16[16,48,768]{2,1,0:T(8,128)(2,1)}), bf16[16,48,768]{2,1,0:T(8,128)(2,1)}, u32[]{:S(2)}, u32[]{:S(2)}) async-start(bf16[16,48,768]{2,1,0:T(8,128)(2,1)} %pad_maximum_fusion.1), calls=%async_computation.2 | async-start | bytes 2359296 | tf_op jit(solution)/shard_map/out_rows/all_to_all | solution.py:644
  178.7 14.7 %attend_backward.2 = (bf16[1024,1152]{1,0:T(8,128)(2,1)S(1)}, f32[3,2,128]{2,1,0:T(2,128)S(1)}) custom-call(bf16[1024,1152]{1,0:T(8,128)(2,1)S(1)} %copy-done.11, bf16[1024,384]{1,0:T(8,128)(2,1)S(1)} %copy-done.33, f32[3,2,1024]{2,1,0:T(2,128)S(1)} %copy-done.38, f32[1024,1]{1,0:T(8,128)S(1)} %copy-done.21), custom_call_target="tpu_custom_call" | custom-call | flops 2518500096 | bytes 1000 | tf_op jit(solution)/shard_map/attend_backward/pallas_call | solution.py:434
  193.4 3.8 %collective-permute-done.25.refs_3_ = bf16[8,48,1536]{2,1,0:T(8,128)(2,1)} collective-permute-done((bf16[8,48,1536]{2,1,0:T(8,128)(2,1)}, bf16[8,48,1536]{2,1,0:T(8,128)(2,1)}, u32[]{:S(2)}, u32[]{:S(2)}) %collective-permute-start.25) | collective-permute-done | bytes 1179680 | tf_op jit(solution)/shard_map/rs_ffn_11/ppermute | solution.py:49
  203.3 7.2 %attend_backward.3 = (bf16[1024,1152]{1,0:T(8,128)(2,1)S(1)}, f32[3,2,128]{2,1,0:T(2,128)S(1)}) custom-call(bf16[1024,1152]{1,0:T(8,128)(2,1)S(1)} %copy-done.11, bf16[1024,384]{1,0:T(8,128)(2,1)S(1)} %copy-done.33, f32[3,2,1024]{2,1,0:T(2,128)S(1)} %copy-done.38, f32[1024,1]{1,0:T(8,128)S(1)} %copy-done.21, ...), custom_call_target="tpu_custom_call", output_to_operand_aliasing={{0}: (4, {}), {1}: (5, {})} | custom-call | flops 1259250048 | bytes 1000 | tf_op jit(solution)/shard_map/attend_backward/pallas_call | solution.py:434
  210.5 4.4 %collective-permute-done.26.refs_1_ = bf16[4,48,1536]{2,1,0:T(8,128)(2,1)S(1)} collective-permute-done((bf16[4,48,1536]{2,1,0:T(8,128)(2,1)S(1)}, bf16[4,48,1536]{2,1,0:T(8,128)(2,1)S(1)}, u32[]{:S(2)}, u32[]{:S(2)}) %collective-permute-start.26) | collective-permute-done | bytes 589856 | tf_op jit(solution)/shard_map/rs_ffn_2/ppermute | solution.py:49
  226.0 6.1 %all-to-all-start.4 = ((bf16[4,48,3072]{2,1,0:T(8,128)(2,1)}), bf16[4,48,3072]{2,1,0:T(8,128)(2,1)}, u32[]{:S(2)}, u32[]{:S(2)}) async-start(bf16[4,48,3072]{2,1,0:T(8,128)(2,1)} %rs_ffn_deal_3.1), calls=%async_computation.4 | async-start | bytes 2359296 | tf_op jit(solution)/shard_map/rs_ffn_3/all_to_all | solution.py:289
  240.0 7.3 %collective-permute-done.30.refs_1_ = bf16[8,48,768]{2,1,0:T(8,128)(2,1)S(1)} collective-permute-done((bf16[8,48,768]{2,1,0:T(8,128)(2,1)}, bf16[8,48,768]{2,1,0:T(8,128)(2,1)S(1)}, u32[]{:S(2)}, u32[]{:S(2)}) %collective-permute-start.30) | collective-permute-done | bytes 589856 | tf_op jit(solution)/shard_map/rs_attn_1/ppermute | solution.py:49
  251.3 4.6 %collective-permute-done.32.refs_1_ = bf16[4,48,768]{2,1,0:T(8,128)(2,1)S(1)} collective-permute-done((bf16[4,48,768]{2,1,0:T(8,128)(2,1)S(1)}, bf16[4,48,768]{2,1,0:T(8,128)(2,1)S(1)}, u32[]{:S(2)}, u32[]{:S(2)}) %collective-permute-start.32) | collective-permute-done | bytes 294944 | tf_op jit(solution)/shard_map/rs_attn_2/ppermute | solution.py:49
  265.0 7.9 %all-to-all-start.3 = ((bf16[16,40,768]{2,1,0:T(8,128)(2,1)}), bf16[16,40,768]{2,1,0:T(8,128)(2,1)S(1)}, u32[]{:S(2)}, u32[]{:S(2)}) async-start(bf16[16,40,768]{2,1,0:T(8,128)(2,1)} %pad_maximum_fusion.2), calls=%async_computation.3 | async-start | bytes 1966080 | tf_op jit(solution)/shard_map/out_rows/all_to_all | solution.py:644
  277.9 15.5 %all-to-all-done.3 = bf16[16,40,768]{2,1,0:T(8,128)(2,1)S(1)} async-done(((bf16[16,40,768]{2,1,0:T(8,128)(2,1)}), bf16[16,40,768]{2,1,0:T(8,128)(2,1)S(1)}, u32[]{:S(2)}, u32[]{:S(2)}) %all-to-all-start.3) | async-done | bytes 983072 | tf_op jit(solution)/shard_map/out_rows/all_to_all | solution.py:644
  (271 shorter events, 125.9 us)
Async XLA Ops:
  7.2 111.5 %all-gather.2.cloned.1.call-start = ((), (), s32[]{:S(2)}) async-start(), calls=%async_computation.5 | async-start | bytes 2506752 | tf_op jit(solution)/shard_map/all_gather | solution.py:732
  8.5 14.5 %collective-permute-start.2 = (bf16[1,48,1152]{2,1,0:T(8,128)(2,1)S(1)}, bf16[1,48,1152]{2,1,0:T(8,128)(2,1)S(1)}, u32[]{:S(2)}, u32[]{:S(2)}) collective-permute-start(bf16[1,48,1152]{2,1,0:T(8,128)(2,1)S(1)} %broadcast_in_dim_reshape.3), channel_id=1, source_target_pairs={{0,24},{2,26},{4,28},{6,30},{8,16},{10,18},{12,20},{14,22},{16,8},... | collective-permute-start | bytes 331784 | tf_op jit(solution)/shard_map/ag_three_first/ppermute | solution.py:49
  22.9 26.6 %all-to-all-start = ((bf16[16,32,768]{2,1,0:T(8,128)(2,1)}), bf16[16,32,768]{2,1,0:T(8,128)(2,1)S(1)}, u32[]{:S(2)}, u32[]{:S(2)}) async-start(bf16[16,32,768]{2,1,0:T(8,128)(2,1)} %gather_fusion), calls=%async_computation | async-start | bytes 1572864 | tf_op jit(solution)/shard_map/in_tokens/all_to_all | solution.py:635
  47.0 15.6 %collective-permute-start.7 = (bf16[8,48,640]{2,1,0:T(8,128)(2,1)S(1)}, bf16[8,48,640]{2,1,0:T(8,128)(2,1)S(1)}, u32[]{:S(2)}, u32[]{:S(2)}) collective-permute-start(bf16[8,48,640]{2,1,0:T(8,128)(2,1)S(1)} %pad_maximum_fusion.6.refs_0_), channel_id=1, source_target_pairs={{0,2},{2,0},{4,6},{6,4},{8,10},{10,8},{12,14},{14,12},{16,18},{18,... | collective-permute-start | bytes 1474568 | tf_op jit(solution)/shard_map/ag_three_last/ppermute | solution.py:49
  49.6 14.7 %collective-permute-start.4 = (bf16[256,768]{1,0:T(8,128)(2,1)S(1)}, bf16[256,768]{1,0:T(8,128)(2,1)S(1)}, u32[]{:S(2)}, u32[]{:S(2)}) collective-permute-start(bf16[256,768]{1,0:T(8,128)(2,1)S(1)} %bitcast.93), channel_id=1, source_target_pairs={{0,1},{1,0},{2,3},{3,2},{4,5},{5,4},{6,7},{7,6},{8,9},{9,8},{10,11... | collective-permute-start | bytes 1179656 | tf_op jit(solution)/shard_map/ppermute | solution.py:49
  49.6 14.6 %collective-permute-start.3 = (bf16[256,768]{1,0:T(8,128)(2,1)S(1)}, bf16[256,768]{1,0:T(8,128)(2,1)S(1)}, u32[]{:S(2)}, u32[]{:S(2)}) collective-permute-start(bf16[256,768]{1,0:T(8,128)(2,1)S(1)} %bitcast.92), channel_id=1, source_target_pairs={{0,1},{1,0},{2,3},{3,2},{4,5},{5,4},{6,7},{7,6},{8,9},{9,8},{10,11... | collective-permute-start | bytes 1179656 | tf_op jit(solution)/shard_map/ppermute | solution.py:49
  50.2 23.8 %collective-permute-start.11 = (bf16[1,48,1920]{2,1,0:T(8,128)(2,1)}, bf16[1,48,1920]{2,1,0:T(8,128)(2,1)S(1)}, u32[]{:S(2)}, u32[]{:S(2)}) collective-permute-start(bf16[1,48,1920]{2,1,0:T(8,128)(2,1)} %bitcast.87), channel_id=1, source_target_pairs={{0,24},{2,26},{4,28},{6,30},{8,16},{10,18},{12,20},{14,22},{16,8},... | collective-permute-start | bytes 552968 | tf_op jit(solution)/shard_map/ag_rest_first/ppermute | solution.py:49
  57.8 17.0 %collective-permute-start.10 = (bf16[1,48,1920]{2,1,0:T(8,128)(2,1)}, bf16[1,48,1920]{2,1,0:T(8,128)(2,1)S(1)}, u32[]{:S(2)}, u32[]{:S(2)}) collective-permute-start(bf16[1,48,1920]{2,1,0:T(8,128)(2,1)} %bitcast.88), channel_id=1, source_target_pairs={{0,16},{2,18},{4,20},{6,22},{8,24},{10,26},{12,28},{14,30},{16,0},... | collective-permute-start | bytes 552968 | tf_op jit(solution)/shard_map/ag_rest_first/ppermute | solution.py:49
  74.9 17.8 %collective-permute-start.12 = (bf16[4,48,1024]{2,1,0:T(8,128)(2,1)S(1)}, bf16[4,48,1024]{2,1,0:T(8,128)(2,1)S(1)}, u32[]{:S(2)}, u32[]{:S(2)}) collective-permute-start(bf16[4,48,1024]{2,1,0:T(8,128)(2,1)S(1)} %slice.136), channel_id=1, source_target_pairs={{0,4},{2,6},{4,0},{6,2},{8,12},{10,14},{12,8},{14,10},{16,20},{18,... | collective-permute-start | bytes 1179656 | tf_op jit(solution)/shard_map/ag_rest_next/ppermute | solution.py:49
  77.2 14.5 %collective-permute-start.13 = (bf16[4,48,896]{2,1,0:T(8,128)(2,1)S(1)}, bf16[4,48,896]{2,1,0:T(8,128)(2,1)S(1)}, u32[]{:S(2)}, u32[]{:S(2)}) collective-permute-start(bf16[4,48,896]{2,1,0:T(8,128)(2,1)S(1)} %slice.137), channel_id=1, source_target_pairs={{0,2},{2,0},{4,6},{6,4},{8,10},{10,8},{12,14},{14,12},{16,18},{18,... | collective-permute-start | bytes 1032200 | tf_op jit(solution)/shard_map/ag_rest_next/ppermute | solution.py:49
  92.9 22.7 %collective-permute-start.14 = (bf16[8,48,1024]{2,1,0:T(8,128)(2,1)S(1)}, bf16[8,48,1024]{2,1,0:T(8,128)(2,1)}, u32[]{:S(2)}, u32[]{:S(2)}) collective-permute-start(bf16[8,48,1024]{2,1,0:T(8,128)(2,1)S(1)} %pad_maximum_fusion.3.refs_0_), channel_id=1, source_target_pairs={{0,2},{2,0},{4,6},{6,4},{8,10},{10,8},{12,14},{14,12},{16,18},{18,... | collective-permute-start | bytes 2359304 | tf_op jit(solution)/shard_map/ag_rest_last/ppermute | solution.py:49
  94.4 21.1 %collective-permute-start.15 = (bf16[8,48,896]{2,1,0:T(8,128)(2,1)S(1)}, bf16[8,48,896]{2,1,0:T(8,128)(2,1)S(1)}, u32[]{:S(2)}, u32[]{:S(2)}) collective-permute-start(bf16[8,48,896]{2,1,0:T(8,128)(2,1)S(1)} %pad_maximum_fusion.5.refs_2_), channel_id=1, source_target_pairs={{0,4},{2,6},{4,0},{6,2},{8,12},{10,14},{12,8},{14,10},{16,20},{18,... | collective-permute-start | bytes 2064392 | tf_op jit(solution)/shard_map/ag_rest_last/ppermute | solution.py:49
  101.3 34.7 %all-to-all-start.1 = ((bf16[16,32,768]{2,1,0:T(8,128)(2,1)}), bf16[16,32,768]{2,1,0:T(8,128)(2,1)}, u32[]{:S(2)}, u32[]{:S(2)}) async-start(bf16[16,32,768]{2,1,0:T(8,128)(2,1)} %gather_fusion.1), calls=%async_computation.1 | async-start | bytes 1572864 | tf_op jit(solution)/shard_map/in_cot/all_to_all | solution.py:635
  156.2 37.1 %collective-permute-start.24 = (bf16[8,48,1536]{2,1,0:T(8,128)(2,1)}, bf16[8,48,1536]{2,1,0:T(8,128)(2,1)}, u32[]{:S(2)}, u32[]{:S(2)}) collective-permute-start(bf16[8,48,1536]{2,1,0:T(8,128)(2,1)} %get-tuple-element.171), channel_id=1, source_target_pairs={{0,2},{2,0},{4,6},{6,4},{8,10},{10,8},{12,14},{14,12},{16,18},{18,... | collective-permute-start | bytes 3538952 | tf_op jit(solution)/shard_map/rs_ffn_10/ppermute | solution.py:49
  160.2 37.0 %collective-permute-start.25 = (bf16[8,48,1536]{2,1,0:T(8,128)(2,1)}, bf16[8,48,1536]{2,1,0:T(8,128)(2,1)}, u32[]{:S(2)}, u32[]{:S(2)}) collective-permute-start(bf16[8,48,1536]{2,1,0:T(8,128)(2,1)} %get-tuple-element.172), channel_id=1, source_target_pairs={{0,4},{2,6},{4,0},{6,2},{8,12},{10,14},{12,8},{14,10},{16,20},{18,... | collective-permute-start | bytes 3538952 | tf_op jit(solution)/shard_map/rs_ffn_11/ppermute | solution.py:49
  168.4 57.6 %all-to-all-start.2 = ((bf16[16,48,768]{2,1,0:T(8,128)(2,1)}), bf16[16,48,768]{2,1,0:T(8,128)(2,1)}, u32[]{:S(2)}, u32[]{:S(2)}) async-start(bf16[16,48,768]{2,1,0:T(8,128)(2,1)} %pad_maximum_fusion.1), calls=%async_computation.2 | async-start | bytes 2359296 | tf_op jit(solution)/shard_map/out_rows/all_to_all | solution.py:644
  199.6 15.3 %collective-permute-start.26 = (bf16[4,48,1536]{2,1,0:T(8,128)(2,1)S(1)}, bf16[4,48,1536]{2,1,0:T(8,128)(2,1)S(1)}, u32[]{:S(2)}, u32[]{:S(2)}) collective-permute-start(bf16[4,48,1536]{2,1,0:T(8,128)(2,1)S(1)} %get-tuple-element.186), channel_id=1, source_target_pairs={{0,4},{2,6},{4,0},{6,2},{8,12},{10,14},{12,8},{14,10},{16,20},{18,... | collective-permute-start | bytes 1769480 | tf_op jit(solution)/shard_map/rs_ffn_2/ppermute | solution.py:49
  201.6 14.5 %collective-permute-start.27 = (bf16[4,48,1536]{2,1,0:T(8,128)(2,1)S(1)}, bf16[4,48,1536]{2,1,0:T(8,128)(2,1)S(1)}, u32[]{:S(2)}, u32[]{:S(2)}) collective-permute-start(bf16[4,48,1536]{2,1,0:T(8,128)(2,1)S(1)} %get-tuple-element.187), channel_id=1, source_target_pairs={{0,2},{2,0},{4,6},{6,4},{8,10},{10,8},{12,14},{14,12},{16,18},{18,... | collective-permute-start | bytes 1769480 | tf_op jit(solution)/shard_map/rs_ffn_2/ppermute | solution.py:49
  226.0 39.0 %all-to-all-start.4 = ((bf16[4,48,3072]{2,1,0:T(8,128)(2,1)}), bf16[4,48,3072]{2,1,0:T(8,128)(2,1)}, u32[]{:S(2)}, u32[]{:S(2)}) async-start(bf16[4,48,3072]{2,1,0:T(8,128)(2,1)} %rs_ffn_deal_3.1), calls=%async_computation.4 | async-start | bytes 2359296 | tf_op jit(solution)/shard_map/rs_ffn_3/all_to_all | solution.py:289
  232.1 15.2 %collective-permute-start.30 = (bf16[8,48,768]{2,1,0:T(8,128)(2,1)}, bf16[8,48,768]{2,1,0:T(8,128)(2,1)S(1)}, u32[]{:S(2)}, u32[]{:S(2)}) collective-permute-start(bf16[8,48,768]{2,1,0:T(8,128)(2,1)} %copy-done.41), channel_id=1, source_target_pairs={{0,2},{2,0},{4,6},{6,4},{8,10},{10,8},{12,14},{14,12},{16,18},{18,... | collective-permute-start | bytes 1769480 | tf_op jit(solution)/shard_map/rs_attn_1/ppermute | solution.py:49
  233.1 14.9 %collective-permute-start.31 = (bf16[8,48,768]{2,1,0:T(8,128)(2,1)}, bf16[8,48,768]{2,1,0:T(8,128)(2,1)S(1)}, u32[]{:S(2)}, u32[]{:S(2)}) collective-permute-start(bf16[8,48,768]{2,1,0:T(8,128)(2,1)} %copy-done.40), channel_id=1, source_target_pairs={{0,4},{2,6},{4,0},{6,2},{8,12},{10,14},{12,8},{14,10},{16,20},{18,... | collective-permute-start | bytes 1769480 | tf_op jit(solution)/shard_map/rs_attn_1/ppermute | solution.py:49
  257.5 15.4 %collective-permute-start.34 = (bf16[1,48,1536]{2,1,0:T(8,128)(2,1)S(1)}, bf16[1,48,1536]{2,1,0:T(8,128)(2,1)S(1)}, u32[]{:S(2)}, u32[]{:S(2)}) collective-permute-start(bf16[1,48,1536]{2,1,0:T(8,128)(2,1)S(1)} %get-tuple-element.220), channel_id=1, source_target_pairs={{0,8},{2,10},{4,12},{6,14},{8,0},{10,2},{12,4},{14,6},{16,24},{18,... | collective-permute-start | bytes 442376 | tf_op jit(solution)/shard_map/rs_attn_3/ppermute | solution.py:49
  259.0 15.0 %collective-permute-start.35 = (bf16[1,48,1536]{2,1,0:T(8,128)(2,1)S(1)}, bf16[1,48,1536]{2,1,0:T(8,128)(2,1)S(1)}, u32[]{:S(2)}, u32[]{:S(2)}) collective-permute-start(bf16[1,48,1536]{2,1,0:T(8,128)(2,1)S(1)} %get-tuple-element.221), channel_id=1, source_target_pairs={{0,16},{2,18},{4,20},{6,22},{8,24},{10,26},{12,28},{14,30},{16,0},... | collective-permute-start | bytes 442376 | tf_op jit(solution)/shard_map/rs_attn_3/ppermute | solution.py:49
  265.0 28.4 %all-to-all-start.3 = ((bf16[16,40,768]{2,1,0:T(8,128)(2,1)}), bf16[16,40,768]{2,1,0:T(8,128)(2,1)S(1)}, u32[]{:S(2)}, u32[]{:S(2)}) async-start(bf16[16,40,768]{2,1,0:T(8,128)(2,1)} %pad_maximum_fusion.2), calls=%async_computation.3 | async-start | bytes 1966080 | tf_op jit(solution)/shard_map/out_rows/all_to_all | solution.py:644
  (73 other events, 503.9 us)
Sparse Core Ops, SparseCore 0:
  14.4 85.4 all-gather.1
where the time goes:
time: 308 us; the launch traced here: 303 us
  Pallas kernels  90.5 us (29%)
  waiting for transfers between devices  83.3 us (27%)
  starting transfers between devices  76.8 us (25%)
  local copies, waits for them, and re-layouts  25.8 us (8%)
  between operations  17.2 us (6%)
  other arithmetic  9.34 us (3%)
    ppermute x39, waiting for transfers between devices, xor_permute(): return lax.ppermute(x, axis, [(i, i ^ mask) for i in range(n)])  63.8 us
    ppermute x39, starting transfers between devices, xor_permute(): return lax.ppermute(x, axis, [(i, i ^ mask) for i in range(n)])  42.2 us
    pallas_call x16, Pallas kernels, call(): pl.pallas_call(kernel, out_shape=[jax.ShapeDtypeStruct(shape, kind) for s...  32.9 us
    pallas_call x2, Pallas kernels, attend_backward(): pl.pallas_call(functools.partial(attend_backward_kernel, min(256, length)...  21.9 us
    pallas_call x3, Pallas kernels, attend_forward(): pl.pallas_call(functools.partial(attend_forward_kernel, min(256, length))...  18 us
    all_to_all x2, starting transfers between devices, exchange_out(): return lax.all_to_all(blocks, 'dp', split_axis=0, concat_axis=0, tiled=True)  17 us
    all_to_all x2, waiting for transfers between devices, exchange_out(): return lax.all_to_all(blocks, 'dp', split_axis=0, concat_axis=0, tiled=True)  15.5 us
    pallas_call x7, Pallas kernels, route(): pl.pallas_call(functools.partial(route_kernel, tuple(plan), kinds, len(ou...  15.4 us
  transfers between devices with their start and end apart: 45, of which 25 were waited for; matrix products, arithmetic and copies ran while one was open for 8% of the time, Pallas kernels for 25%

commit v1 on v0

--- a/solution.py
+++ b/solution.py
@@ -57,6 +57,14 @@
         out.append((at, 1 << width))
         at += width
     return out[::-1]
+
+
+def pairs_of(axes):
+    out = []
+    for shift, size in axes:
+        width = size.bit_length() - 1
+        out += [(shift + bit, 2) for bit in reversed(range(width))]
+    return out
 
 
 def stage_parts(x, shift, size):
@@ -702,6 +710,7 @@
     high = axes[:-2]
     order_one = high + low
     order_two = high + low[::-1]
+    high_two = pairs_of(high)
     back_one = low[::-1] + high[::-1]
     back_two = low + high[::-1]
 
@@ -813,7 +822,10 @@
         scratch=[pltpu.VMEM(big, BF16)],
     )
     ffn = Scatter(
-        [[(gradient(grad_two_low, hidden_low), 0, hidden_cols)], None], [back_one, back_two], axes, "rs_ffn", True
+        [[(gradient(grad_two_low, hidden_low), 0, hidden_cols)], None],
+        [low[::-1] + high_two[::-1], low + high_two[::-1]],
+        high_two + low,
+        "rs_ffn",
     )
     dealt = ffn.deal_one(0)
     grad_two_low, dealt = lax.optimization_barrier((grad_two_low, dealt))
@@ -865,8 +877,8 @@
             [(grad_w_three, 0, cut)],
             [(grad_w_three, cut, 3 * head_cols), (grad_w_back, 0, head_cols)],
         ],
-        [back_one, back_two],
-        axes,
+        [low[::-1] + high_two[::-1], low + high_two[::-1]],
+        high_two + low,
         "rs_attn",
     )
     tail.deal()
@@ -880,7 +892,6 @@
         2.3,
     )
     got = from_other(sent)
-    got, sent_tokens = lax.optimization_barrier((got, sent_tokens))
     grad_in, late = call(
         functools.partial(late_kernel, pairs),
         [((half_len, width), BF16), ((8, 2 * head_cols), BF16)],
@@ -892,6 +903,11 @@
     block = half_len // dp_size
     out_tokens, early_all = taken_out(sent_tokens, block)
     out_grad, late_all = taken_out(sent_grad, block)
+    tail.deal()
+    ffn.deal()
+    tail.dealt, ffn.dealt = lax.optimization_barrier((tail.dealt, ffn.dealt))
+    ffn.send()
+    tail.send()
     ffn_sum = ffn.finish()
     down_sum, up_sum = ffn_sum[:, :hidden_cols], ffn_sum[:, hidden_cols:]
     attn_sum = tail.finish()

time: 308 us -> 298 us (0.968)
  starting transfers between devices: 76.8 us -> 70.1 us
    all_to_all x2, waiting for transfers between devices: 15.5 us -> 0.01 us  [exchange_out(): return lax.all_to_all(blocks, 'dp', split_axis=0, concat_axis=0, tiled=True)]
    ppermute x39 -> x40, waiting for transfers between devices: 63.8 us -> 78.2 us  [xor_permute(): return lax.ppermute(x, axis, [(i, i ^ mask) for i in range(n)])]
    all_to_all x1 -> x0, starting transfers between devices: 6.08 us -> none  [send(): lax.all_to_all(parts[0], 'dp', split_axis=0, concat_axis=0, axis_index_gr...]
    unnamed x114 -> x110, local copies, waits for them, and re-layouts: 12.4 us -> 11 us
    pallas_call x7 -> x9, Pallas kernels: 15.4 us -> 16.4 us  [route(): pl.pallas_call(functools.partial(route_kernel, tuple(plan), kinds, len(ou...]
    ppermute x39 -> x40, starting transfers between devices: 42.2 us -> 42.1 us  [xor_permute(): return lax.ppermute(x, axis, [(i, i ^ mask) for i in range(n)])]
  transfers between devices with their start and end apart: 45 -> 45, of which waited for: 25 -> 24; matrix products, arithmetic and copies ran while one was open for 8% -> 8% of each run, Pallas kernels for 25% -> 26%
where the time goes in v1:
time: 298 us; the launch traced here: 293 us
  Pallas kernels  91.5 us (31%)
  waiting for transfers between devices  80.4 us (27%)
  starting transfers between devices  70.1 us (24%)
  local copies, waits for them, and re-layouts  25.5 us (9%)
  between operations  17.2 us (6%)
  other arithmetic  7.99 us (3%)
    ppermute x40, waiting for transfers between devices, xor_permute(): return lax.ppermute(x, axis, [(i, i ^ mask) for i in range(n)])  78.2 us
    ppermute x40, starting transfers between devices, xor_permute(): return lax.ppermute(x, axis, [(i, i ^ mask) for i in range(n)])  42.1 us
    pallas_call x16, Pallas kernels, call(): pl.pallas_call(kernel, out_shape=[jax.ShapeDtypeStruct(shape, kind) for s...  32.9 us
    pallas_call x2, Pallas kernels, attend_backward(): pl.pallas_call(functools.partial(attend_backward_kernel, min(256, length)...  21.9 us
    pallas_call x3, Pallas kernels, attend_forward(): pl.pallas_call(functools.partial(attend_forward_kernel, min(256, length))...  18 us
    all_to_all x2, starting transfers between devices, exchange_out(): return lax.all_to_all(blocks, 'dp', split_axis=0, concat_axis=0, tiled=True)  16.5 us
    pallas_call x9, Pallas kernels, route(): pl.pallas_call(functools.partial(route_kernel, tuple(plan), kinds, len(ou...  16.4 us
    all_to_all x2, starting transfers between devices, exchange_in(): lax.all_to_all(dealt, 'dp', split_axis=0, concat_axis=0, tiled=True)  11.4 us
  transfers between devices with their start and end apart: 45, of which 24 were waited for; matrix products, arithmetic and copies ran while one was open for 8% of the time, Pallas kernels for 26%

profile of v1, /device:TPU:0, one launch (start us, length us, event | category | flops | bytes accessed | tf_op | source)
XLA Modules:
  0.0 292.7 jit_solution(14149353145512842056)
XLA Ops:
  8.5 5.1 %collective-permute-start.2 = (bf16[1,48,1152]{2,1,0:T(8,128)(2,1)S(1)}, bf16[1,48,1152]{2,1,0:T(8,128)(2,1)S(1)}, u32[]{:S(2)}, u32[]{:S(2)}) collective-permute-start(bf16[1,48,1152]{2,1,0:T(8,128)(2,1)S(1)} %broadcast_in_dim_reshape.3), channel_id=1, source_target_pairs={{0,24},{2,26},{4,28},{6,30},{8,16},{10,18},{12,20},{14,22},{16,8},... | collective-permute-start | bytes 331784 | tf_op jit(solution)/shard_map/ag_three_first/ppermute | solution.py:49
  22.9 5.8 %all-to-all-start = ((bf16[16,32,768]{2,1,0:T(8,128)(2,1)}), bf16[16,32,768]{2,1,0:T(8,128)(2,1)S(1)}, u32[]{:S(2)}, u32[]{:S(2)}) async-start(bf16[16,32,768]{2,1,0:T(8,128)(2,1)} %gather_fusion), calls=%async_computation | async-start | bytes 1572864 | tf_op jit(solution)/shard_map/in_tokens/all_to_all | solution.py:643
  40.1 3.9 %collective-permute-done.5 = bf16[4,48,640]{2,1,0:T(8,128)(2,1)S(1)} collective-permute-done((bf16[4,48,640]{2,1,0:T(8,128)(2,1)S(1)}, bf16[4,48,640]{2,1,0:T(8,128)(2,1)S(1)}, u32[]{:S(2)}, u32[]{:S(2)}) %collective-permute-start.5) | collective-permute-done | bytes 245792 | tf_op jit(solution)/shard_map/ag_three_next/ppermute | solution.py:49
  50.2 5.0 %collective-permute-start.11 = (bf16[1,48,1920]{2,1,0:T(8,128)(2,1)}, bf16[1,48,1920]{2,1,0:T(8,128)(2,1)S(1)}, u32[]{:S(2)}, u32[]{:S(2)}) collective-permute-start(bf16[1,48,1920]{2,1,0:T(8,128)(2,1)} %bitcast.87), channel_id=1, source_target_pairs={{0,24},{2,26},{4,28},{6,30},{8,16},{10,18},{12,20},{14,22},{16,8},... | collective-permute-start | bytes 552968 | tf_op jit(solution)/shard_map/ag_rest_first/ppermute | solution.py:49
  68.1 5.9 %attend_forward.3 = (bf16[1024,384]{1,0:T(8,128)(2,1)S(1)}, f32[3,2,1024]{2,1,0:T(2,128)S(1)}) custom-call(bf16[1024,1152]{1,0:T(8,128)(2,1)S(1)} %project.1.qkv_ref, f32[1024,1]{1,0:T(8,128)S(1)} %fusion.5.bias_ref), custom_call_target="tpu_custom_call" | custom-call | flops 1017750016 | bytes 1000 | tf_op jit(solution)/shard_map/attend_forward/pallas_call | solution.py:380
  78.0 5.9 %attend_forward.4 = (bf16[1024,384]{1,0:T(8,128)(2,1)S(1)}, f32[3,2,1024]{2,1,0:T(2,128)S(1)}) custom-call(bf16[1024,1152]{1,0:T(8,128)(2,1)S(1)} %project.1.qkv_ref, f32[1024,1]{1,0:T(8,128)S(1)} %fusion.5.bias_ref, bf16[1024,384]{1,0:T(8,128)(2,1)S(1)} %get-tuple-element.138.refs_0_, ...), custom_call_target="tpu_custom_call", output_to_operand_aliasing={{0}: (2, {}), {1}: (3, {})} | custom-call | flops 1017750016 | bytes 1000 | tf_op jit(solution)/shard_map/attend_forward/pallas_call | solution.py:380
  83.9 7.8 %collective-permute-done.13 = bf16[4,48,896]{2,1,0:T(8,128)(2,1)S(1)} collective-permute-done((bf16[4,48,896]{2,1,0:T(8,128)(2,1)S(1)}, bf16[4,48,896]{2,1,0:T(8,128)(2,1)S(1)}, u32[]{:S(2)}, u32[]{:S(2)}) %collective-permute-start.13) | collective-permute-done | bytes 344096 | tf_op jit(solution)/shard_map/ag_rest_next/ppermute | solution.py:49
  95.0 6.3 %attend_forward.5 = (bf16[1024,384]{1,0:T(8,128)(2,1)S(1)}, f32[3,2,1024]{2,1,0:T(2,128)S(1)}) custom-call(bf16[1024,1152]{1,0:T(8,128)(2,1)S(1)} %project.1.qkv_ref, f32[1024,1]{1,0:T(8,128)S(1)} %fusion.5.bias_ref, bf16[1024,384]{1,0:T(8,128)(2,1)S(1)} %get-tuple-element.147.refs_0_, ...), custom_call_target="tpu_custom_call", output_to_operand_aliasing={{0}: (2, {}), {1}: (3, {})} | custom-call | flops 1017750016 | bytes 1000 | tf_op jit(solution)/shard_map/attend_forward/pallas_call | solution.py:380
  101.3 5.7 %all-to-all-start.1 = ((bf16[16,32,768]{2,1,0:T(8,128)(2,1)}), bf16[16,32,768]{2,1,0:T(8,128)(2,1)}, u32[]{:S(2)}, u32[]{:S(2)}) async-start(bf16[16,32,768]{2,1,0:T(8,128)(2,1)} %gather_fusion.1), calls=%async_computation.1 | async-start | bytes 1572864 | tf_op jit(solution)/shard_map/in_cot/all_to_all | solution.py:643
  107.0 8.6 %collective-permute-done.15.refs_3_ = bf16[8,48,896]{2,1,0:T(8,128)(2,1)S(1)} collective-permute-done((bf16[8,48,896]{2,1,0:T(8,128)(2,1)S(1)}, bf16[8,48,896]{2,1,0:T(8,128)(2,1)S(1)}, u32[]{:S(2)}, u32[]{:S(2)}) %collective-permute-start.15) | collective-permute-done | bytes 688160 | tf_op jit(solution)/shard_map/ag_rest_last/ppermute | solution.py:49
  123.5 6.1 %middle.1 = (bf16[1024,768]{1,0:T(8,128)(2,1)S(1)}, f32[1024,1]{1,0:T(8,128)S(1)}, bf16[1024,768]{1,0:T(8,128)(2,1)S(1)}, bf16[1024,1536]{1,0:T(8,128)(2,1)S(1)}, bf16[1024,1536]{1,0:T(8,128)(2,1)S(1)}) custom-call(bf16[1024,768]{1,0:T(8,128)(2,1)S(1)} %copy-done.1, bf16[512,768]{1,0:T(8,128)(2,1)S(1)} %attn_part_0.1.p0, ...), custom_call_target="tpu_custom_call" | custom-call | flops 1380000000 | bytes 1000 | tf_op jit(solution)/shard_map/middle/pallas_call | solution.py:470
  140.1 5.5 %outer.1 = (bf16[512,768]{1,0:T(8,128)(2,1)S(1)}, bf16[1024,768]{1,0:T(8,128)(2,1)S(1)}, f32[3,768]{1,0:T(4,128)S(1)}) custom-call(bf16[1024,768]{1,0:T(8,128)(2,1)S(1)} %copy-done.15, bf16[512,768]{1,0:T(8,128)(2,1)} %ffn_part_0.1.p0, bf16[512,768]{1,0:T(8,128)(2,1)} %ffn_part_1.1.p1, bf16[512,768]{1,0:T(8,128)(2,1)} %collective-permute-done.18.p2, ...), custom_call_target="tpu_custom_call" | custom-call | flops 776249984 | bytes 1000 | tf_op jit(solution)/shard_map/outer/pallas_call | solution.py:470
  145.6 3.8 %rs_ffn_deal_10.1 = (bf16[8,48,1536]{2,1,0:T(8,128)(2,1)S(1)}, bf16[8,48,1536]{2,1,0:T(8,128)(2,1)}) custom-call(bf16[1024,768]{1,0:T(8,128)(2,1)S(1)} %get-tuple-element.168.refs_0_.grad_ref.grad_in_ref, bf16[1024,1536]{1,0:T(8,128)(2,1)S(1)} %get-tuple-element.161.x_ref.refs_1_), custom_call_target="tpu_custom_call" | custom-call | flops 172500000 | bytes 1000 | tf_op jit(solution)/shard_map/rs_ffn_deal_10/pallas_call | solution.py:237
  156.2 3.9 %rs_ffn_deal_11.1 = (bf16[8,48,1536]{2,1,0:T(8,128)(2,1)S(1)}, bf16[8,48,1536]{2,1,0:T(8,128)(2,1)}) custom-call(bf16[1024,768]{1,0:T(8,128)(2,1)S(1)} %copy-done.27, bf16[1024,1536]{1,0:T(8,128)(2,1)S(1)} %get-tuple-element.173.x_ref.refs_1_), custom_call_target="tpu_custom_call" | custom-call | flops 172500000 | bytes 1000 | tf_op jit(solution)/shard_map/rs_ffn_deal_11/pallas_call | solution.py:237
  168.4 9.1 %all-to-all-start.2 = ((bf16[16,48,768]{2,1,0:T(8,128)(2,1)}), bf16[16,48,768]{2,1,0:T(8,128)(2,1)}, u32[]{:S(2)}, u32[]{:S(2)}) async-start(bf16[16,48,768]{2,1,0:T(8,128)(2,1)} %pad_maximum_fusion.1), calls=%async_computation.2 | async-start | bytes 2359296 | tf_op jit(solution)/shard_map/out_rows/all_to_all | solution.py:652
  178.7 14.7 %attend_backward.2 = (bf16[1024,1152]{1,0:T(8,128)(2,1)S(1)}, f32[3,2,128]{2,1,0:T(2,128)S(1)}) custom-call(bf16[1024,1152]{1,0:T(8,128)(2,1)S(1)} %copy-done.11, bf16[1024,384]{1,0:T(8,128)(2,1)S(1)} %copy-done.33, f32[3,2,1024]{2,1,0:T(2,128)S(1)} %copy-done.38, f32[1024,1]{1,0:T(8,128)S(1)} %copy-done.21), custom_call_target="tpu_custom_call" | custom-call | flops 2518500096 | bytes 1000 | tf_op jit(solution)/shard_map/attend_backward/pallas_call | solution.py:442
  193.4 3.8 %collective-permute-done.25.refs_3_ = bf16[8,48,1536]{2,1,0:T(8,128)(2,1)} collective-permute-done((bf16[8,48,1536]{2,1,0:T(8,128)(2,1)}, bf16[8,48,1536]{2,1,0:T(8,128)(2,1)}, u32[]{:S(2)}, u32[]{:S(2)}) %collective-permute-start.25) | collective-permute-done | bytes 1179680 | tf_op jit(solution)/shard_map/rs_ffn_11/ppermute | solution.py:49
  203.3 7.2 %attend_backward.3 = (bf16[1024,1152]{1,0:T(8,128)(2,1)S(1)}, f32[3,2,128]{2,1,0:T(2,128)S(1)}) custom-call(bf16[1024,1152]{1,0:T(8,128)(2,1)S(1)} %copy-done.11, bf16[1024,384]{1,0:T(8,128)(2,1)S(1)} %copy-done.33, f32[3,2,1024]{2,1,0:T(2,128)S(1)} %copy-done.38, f32[1024,1]{1,0:T(8,128)S(1)} %copy-done.21, ...), custom_call_target="tpu_custom_call", output_to_operand_aliasing={{0}: (4, {}), {1}: (5, {})} | custom-call | flops 1259250048 | bytes 1000 | tf_op jit(solution)/shard_map/attend_backward/pallas_call | solution.py:442
  210.5 4.4 %collective-permute-done.26.refs_1_ = bf16[4,48,1536]{2,1,0:T(8,128)(2,1)S(1)} collective-permute-done((bf16[4,48,1536]{2,1,0:T(8,128)(2,1)S(1)}, bf16[4,48,1536]{2,1,0:T(8,128)(2,1)S(1)}, u32[]{:S(2)}, u32[]{:S(2)}) %collective-permute-start.26) | collective-permute-done | bytes 589856 | tf_op jit(solution)/shard_map/rs_ffn_2/ppermute | solution.py:49
  217.2 4.4 %rs_attn_deal_1.1 = (bf16[8,48,768]{2,1,0:T(8,128)(2,1)S(1)}, bf16[8,48,768]{2,1,0:T(8,128)(2,1)}, bf16[8,48,768]{2,1,0:T(8,128)(2,1)S(1)}, bf16[8,48,768]{2,1,0:T(8,128)(2,1)}) custom-call(bf16[1024,768]{1,0:T(8,128)(2,1)S(1)} %copy-done.2, bf16[1024,1152]{1,0:T(8,128)(2,1)S(1)} %get-tuple-element.212.refs_1_.x_ref, bf16[1024,768]{1,0:T(8,128)(2,1)S(1)} %copy-done.25, ...), custom_call_target="tpu_custom_call" | custom-call | flops 172500000 | bytes 1000 | tf_op jit(solution)/shard_map/rs_attn_deal_1/pallas_call | solution.py:237
  228.2 7.4 %all-to-all-start.3 = ((bf16[16,40,768]{2,1,0:T(8,128)(2,1)}), bf16[16,40,768]{2,1,0:T(8,128)(2,1)}, u32[]{:S(2)}, u32[]{:S(2)}) async-start(bf16[16,40,768]{2,1,0:T(8,128)(2,1)} %pad_maximum_fusion.2), calls=%async_computation.3 | async-start | bytes 1966080 | tf_op jit(solution)/shard_map/out_rows/all_to_all | solution.py:652
  240.7 8.8 %collective-permute-done.32.refs_1_ = bf16[2,48,3072]{2,1,0:T(8,128)(2,1)S(1)} collective-permute-done((bf16[2,48,3072]{2,1,0:T(8,128)(2,1)}, bf16[2,48,3072]{2,1,0:T(8,128)(2,1)S(1)}, u32[]{:S(2)}, u32[]{:S(2)}) %collective-permute-start.32) | collective-permute-done | bytes 589856 | tf_op jit(solution)/shard_map/rs_ffn_3/ppermute | solution.py:49
  254.3 3.8 %collective-permute-done.33.refs_1_ = bf16[4,48,768]{2,1,0:T(8,128)(2,1)S(1)} collective-permute-done((bf16[4,48,768]{2,1,0:T(8,128)(2,1)S(1)}, bf16[4,48,768]{2,1,0:T(8,128)(2,1)S(1)}, u32[]{:S(2)}, u32[]{:S(2)}) %collective-permute-start.33) | collective-permute-done | bytes 294944 | tf_op jit(solution)/shard_map/rs_attn_2/ppermute | solution.py:49
  261.1 11.5 %collective-permute-done.37 = bf16[1,48,3072]{2,1,0:T(8,128)(2,1)S(1)} collective-permute-done((bf16[1,48,3072]{2,1,0:T(8,128)(2,1)S(1)}, bf16[1,48,3072]{2,1,0:T(8,128)(2,1)S(1)}, u32[]{:S(2)}, u32[]{:S(2)}) %collective-permute-start.37) | collective-permute-done | bytes 294944 | tf_op jit(solution)/shard_map/rs_ffn_4/ppermute | solution.py:49
  (269 shorter events, 121.1 us)
Async XLA Ops:
  7.2 111.5 %all-gather.2.cloned.1.call-start = ((), (), s32[]{:S(2)}) async-start(), calls=%async_computation.4 | async-start | bytes 2506752 | tf_op jit(solution)/shard_map/all_gather | solution.py:741
  8.5 14.5 %collective-permute-start.2 = (bf16[1,48,1152]{2,1,0:T(8,128)(2,1)S(1)}, bf16[1,48,1152]{2,1,0:T(8,128)(2,1)S(1)}, u32[]{:S(2)}, u32[]{:S(2)}) collective-permute-start(bf16[1,48,1152]{2,1,0:T(8,128)(2,1)S(1)} %broadcast_in_dim_reshape.3), channel_id=1, source_target_pairs={{0,24},{2,26},{4,28},{6,30},{8,16},{10,18},{12,20},{14,22},{16,8},... | collective-permute-start | bytes 331784 | tf_op jit(solution)/shard_map/ag_three_first/ppermute | solution.py:49
  22.9 26.6 %all-to-all-start = ((bf16[16,32,768]{2,1,0:T(8,128)(2,1)}), bf16[16,32,768]{2,1,0:T(8,128)(2,1)S(1)}, u32[]{:S(2)}, u32[]{:S(2)}) async-start(bf16[16,32,768]{2,1,0:T(8,128)(2,1)} %gather_fusion), calls=%async_computation | async-start | bytes 1572864 | tf_op jit(solution)/shard_map/in_tokens/all_to_all | solution.py:643
  44.1 13.7 %collective-permute-start.8 = (bf16[8,48,512]{2,1,0:T(8,128)(2,1)S(1)}, bf16[8,48,512]{2,1,0:T(8,128)(2,1)S(1)}, u32[]{:S(2)}, u32[]{:S(2)}) collective-permute-start(bf16[8,48,512]{2,1,0:T(8,128)(2,1)S(1)} %pad_maximum_fusion.7.refs_2_), channel_id=1, source_target_pairs={{0,4},{2,6},{4,0},{6,2},{8,12},{10,14},{12,8},{14,10},{16,20},{18,... | collective-permute-start | bytes 1179656 | tf_op jit(solution)/shard_map/ag_three_last/ppermute | solution.py:49
  47.0 15.6 %collective-permute-start.7 = (bf16[8,48,640]{2,1,0:T(8,128)(2,1)S(1)}, bf16[8,48,640]{2,1,0:T(8,128)(2,1)S(1)}, u32[]{:S(2)}, u32[]{:S(2)}) collective-permute-start(bf16[8,48,640]{2,1,0:T(8,128)(2,1)S(1)} %pad_maximum_fusion.6.refs_0_), channel_id=1, source_target_pairs={{0,2},{2,0},{4,6},{6,4},{8,10},{10,8},{12,14},{14,12},{16,18},{18,... | collective-permute-start | bytes 1474568 | tf_op jit(solution)/shard_map/ag_three_last/ppermute | solution.py:49
  49.6 14.7 %collective-permute-start.4 = (bf16[256,768]{1,0:T(8,128)(2,1)S(1)}, bf16[256,768]{1,0:T(8,128)(2,1)S(1)}, u32[]{:S(2)}, u32[]{:S(2)}) collective-permute-start(bf16[256,768]{1,0:T(8,128)(2,1)S(1)} %bitcast.93), channel_id=1, source_target_pairs={{0,1},{1,0},{2,3},{3,2},{4,5},{5,4},{6,7},{7,6},{8,9},{9,8},{10,11... | collective-permute-start | bytes 1179656 | tf_op jit(solution)/shard_map/ppermute | solution.py:49
  49.6 14.6 %collective-permute-start.3 = (bf16[256,768]{1,0:T(8,128)(2,1)S(1)}, bf16[256,768]{1,0:T(8,128)(2,1)S(1)}, u32[]{:S(2)}, u32[]{:S(2)}) collective-permute-start(bf16[256,768]{1,0:T(8,128)(2,1)S(1)} %bitcast.92), channel_id=1, source_target_pairs={{0,1},{1,0},{2,3},{3,2},{4,5},{5,4},{6,7},{7,6},{8,9},{9,8},{10,11... | collective-permute-start | bytes 1179656 | tf_op jit(solution)/shard_map/ppermute | solution.py:49
  50.2 23.8 %collective-permute-start.11 = (bf16[1,48,1920]{2,1,0:T(8,128)(2,1)}, bf16[1,48,1920]{2,1,0:T(8,128)(2,1)S(1)}, u32[]{:S(2)}, u32[]{:S(2)}) collective-permute-start(bf16[1,48,1920]{2,1,0:T(8,128)(2,1)} %bitcast.87), channel_id=1, source_target_pairs={{0,24},{2,26},{4,28},{6,30},{8,16},{10,18},{12,20},{14,22},{16,8},... | collective-permute-start | bytes 552968 | tf_op jit(solution)/shard_map/ag_rest_first/ppermute | solution.py:49
  57.8 17.0 %collective-permute-start.10 = (bf16[1,48,1920]{2,1,0:T(8,128)(2,1)}, bf16[1,48,1920]{2,1,0:T(8,128)(2,1)S(1)}, u32[]{:S(2)}, u32[]{:S(2)}) collective-permute-start(bf16[1,48,1920]{2,1,0:T(8,128)(2,1)} %bitcast.88), channel_id=1, source_target_pairs={{0,16},{2,18},{4,20},{6,22},{8,24},{10,26},{12,28},{14,30},{16,0},... | collective-permute-start | bytes 552968 | tf_op jit(solution)/shard_map/ag_rest_first/ppermute | solution.py:49
  74.9 17.8 %collective-permute-start.12 = (bf16[4,48,1024]{2,1,0:T(8,128)(2,1)S(1)}, bf16[4,48,1024]{2,1,0:T(8,128)(2,1)S(1)}, u32[]{:S(2)}, u32[]{:S(2)}) collective-permute-start(bf16[4,48,1024]{2,1,0:T(8,128)(2,1)S(1)} %slice.124), channel_id=1, source_target_pairs={{0,4},{2,6},{4,0},{6,2},{8,12},{10,14},{12,8},{14,10},{16,20},{18,... | collective-permute-start | bytes 1179656 | tf_op jit(solution)/shard_map/ag_rest_next/ppermute | solution.py:49
  77.2 14.5 %collective-permute-start.13 = (bf16[4,48,896]{2,1,0:T(8,128)(2,1)S(1)}, bf16[4,48,896]{2,1,0:T(8,128)(2,1)S(1)}, u32[]{:S(2)}, u32[]{:S(2)}) collective-permute-start(bf16[4,48,896]{2,1,0:T(8,128)(2,1)S(1)} %slice.125), channel_id=1, source_target_pairs={{0,2},{2,0},{4,6},{6,4},{8,10},{10,8},{12,14},{14,12},{16,18},{18,... | collective-permute-start | bytes 1032200 | tf_op jit(solution)/shard_map/ag_rest_next/ppermute | solution.py:49
  92.9 22.7 %collective-permute-start.14 = (bf16[8,48,1024]{2,1,0:T(8,128)(2,1)S(1)}, bf16[8,48,1024]{2,1,0:T(8,128)(2,1)}, u32[]{:S(2)}, u32[]{:S(2)}) collective-permute-start(bf16[8,48,1024]{2,1,0:T(8,128)(2,1)S(1)} %pad_maximum_fusion.3.refs_0_), channel_id=1, source_target_pairs={{0,2},{2,0},{4,6},{6,4},{8,10},{10,8},{12,14},{14,12},{16,18},{18,... | collective-permute-start | bytes 2359304 | tf_op jit(solution)/shard_map/ag_rest_last/ppermute | solution.py:49
  94.4 21.1 %collective-permute-start.15 = (bf16[8,48,896]{2,1,0:T(8,128)(2,1)S(1)}, bf16[8,48,896]{2,1,0:T(8,128)(2,1)S(1)}, u32[]{:S(2)}, u32[]{:S(2)}) collective-permute-start(bf16[8,48,896]{2,1,0:T(8,128)(2,1)S(1)} %pad_maximum_fusion.5.refs_2_), channel_id=1, source_target_pairs={{0,4},{2,6},{4,0},{6,2},{8,12},{10,14},{12,8},{14,10},{16,20},{18,... | collective-permute-start | bytes 2064392 | tf_op jit(solution)/shard_map/ag_rest_last/ppermute | solution.py:49
  101.3 34.7 %all-to-all-start.1 = ((bf16[16,32,768]{2,1,0:T(8,128)(2,1)}), bf16[16,32,768]{2,1,0:T(8,128)(2,1)}, u32[]{:S(2)}, u32[]{:S(2)}) async-start(bf16[16,32,768]{2,1,0:T(8,128)(2,1)} %gather_fusion.1), calls=%async_computation.1 | async-start | bytes 1572864 | tf_op jit(solution)/shard_map/in_cot/all_to_all | solution.py:643
  156.2 37.1 %collective-permute-start.24 = (bf16[8,48,1536]{2,1,0:T(8,128)(2,1)}, bf16[8,48,1536]{2,1,0:T(8,128)(2,1)}, u32[]{:S(2)}, u32[]{:S(2)}) collective-permute-start(bf16[8,48,1536]{2,1,0:T(8,128)(2,1)} %get-tuple-element.183), channel_id=1, source_target_pairs={{0,2},{2,0},{4,6},{6,4},{8,10},{10,8},{12,14},{14,12},{16,18},{18,... | collective-permute-start | bytes 3538952 | tf_op jit(solution)/shard_map/rs_ffn_10/ppermute | solution.py:49
  160.2 37.0 %collective-permute-start.25 = (bf16[8,48,1536]{2,1,0:T(8,128)(2,1)}, bf16[8,48,1536]{2,1,0:T(8,128)(2,1)}, u32[]{:S(2)}, u32[]{:S(2)}) collective-permute-start(bf16[8,48,1536]{2,1,0:T(8,128)(2,1)} %get-tuple-element.184), channel_id=1, source_target_pairs={{0,4},{2,6},{4,0},{6,2},{8,12},{10,14},{12,8},{14,10},{16,20},{18,... | collective-permute-start | bytes 3538952 | tf_op jit(solution)/shard_map/rs_ffn_11/ppermute | solution.py:49
  168.4 59.8 %all-to-all-start.2 = ((bf16[16,48,768]{2,1,0:T(8,128)(2,1)}), bf16[16,48,768]{2,1,0:T(8,128)(2,1)}, u32[]{:S(2)}, u32[]{:S(2)}) async-start(bf16[16,48,768]{2,1,0:T(8,128)(2,1)} %pad_maximum_fusion.1), calls=%async_computation.2 | async-start | bytes 2359296 | tf_op jit(solution)/shard_map/out_rows/all_to_all | solution.py:652
  199.7 15.3 %collective-permute-start.26 = (bf16[4,48,1536]{2,1,0:T(8,128)(2,1)S(1)}, bf16[4,48,1536]{2,1,0:T(8,128)(2,1)S(1)}, u32[]{:S(2)}, u32[]{:S(2)}) collective-permute-start(bf16[4,48,1536]{2,1,0:T(8,128)(2,1)S(1)} %get-tuple-element.198), channel_id=1, source_target_pairs={{0,4},{2,6},{4,0},{6,2},{8,12},{10,14},{12,8},{14,10},{16,20},{18,... | collective-permute-start | bytes 1769480 | tf_op jit(solution)/shard_map/rs_ffn_2/ppermute | solution.py:49
  201.6 14.5 %collective-permute-start.27 = (bf16[4,48,1536]{2,1,0:T(8,128)(2,1)S(1)}, bf16[4,48,1536]{2,1,0:T(8,128)(2,1)S(1)}, u32[]{:S(2)}, u32[]{:S(2)}) collective-permute-start(bf16[4,48,1536]{2,1,0:T(8,128)(2,1)S(1)} %get-tuple-element.199), channel_id=1, source_target_pairs={{0,2},{2,0},{4,6},{6,4},{8,10},{10,8},{12,14},{14,12},{16,18},{18,... | collective-permute-start | bytes 1769480 | tf_op jit(solution)/shard_map/rs_ffn_2/ppermute | solution.py:49
  224.5 25.2 %collective-permute-start.30 = (bf16[8,48,768]{2,1,0:T(8,128)(2,1)}, bf16[8,48,768]{2,1,0:T(8,128)(2,1)S(1)}, u32[]{:S(2)}, u32[]{:S(2)}) collective-permute-start(bf16[8,48,768]{2,1,0:T(8,128)(2,1)} %get-tuple-element.219), channel_id=1, source_target_pairs={{0,2},{2,0},{4,6},{6,4},{8,10},{10,8},{12,14},{14,12},{16,18},{18,... | collective-permute-start | bytes 1769480 | tf_op jit(solution)/shard_map/rs_attn_1/ppermute | solution.py:49
  225.6 24.0 %collective-permute-start.31 = (bf16[8,48,768]{2,1,0:T(8,128)(2,1)}, bf16[8,48,768]{2,1,0:T(8,128)(2,1)S(1)}, u32[]{:S(2)}, u32[]{:S(2)}) collective-permute-start(bf16[8,48,768]{2,1,0:T(8,128)(2,1)} %get-tuple-element.221), channel_id=1, source_target_pairs={{0,4},{2,6},{4,0},{6,2},{8,12},{10,14},{12,8},{14,10},{16,20},{18,... | collective-permute-start | bytes 1769480 | tf_op jit(solution)/shard_map/rs_attn_1/ppermute | solution.py:49
  226.5 23.0 %collective-permute-start.32 = (bf16[2,48,3072]{2,1,0:T(8,128)(2,1)}, bf16[2,48,3072]{2,1,0:T(8,128)(2,1)S(1)}, u32[]{:S(2)}, u32[]{:S(2)}) collective-permute-start(bf16[2,48,3072]{2,1,0:T(8,128)(2,1)} %get-tuple-element.227), channel_id=1, source_target_pairs={{0,8},{2,10},{4,12},{6,14},{8,0},{10,2},{12,4},{14,6},{16,24},{18,... | collective-permute-start | bytes 1769480 | tf_op jit(solution)/shard_map/rs_ffn_3/ppermute | solution.py:49
  228.2 53.0 %all-to-all-start.3 = ((bf16[16,40,768]{2,1,0:T(8,128)(2,1)}), bf16[16,40,768]{2,1,0:T(8,128)(2,1)}, u32[]{:S(2)}, u32[]{:S(2)}) async-start(bf16[16,40,768]{2,1,0:T(8,128)(2,1)} %pad_maximum_fusion.2), calls=%async_computation.3 | async-start | bytes 1966080 | tf_op jit(solution)/shard_map/out_rows/all_to_all | solution.py:652
  251.3 21.3 %collective-permute-start.37 = (bf16[1,48,3072]{2,1,0:T(8,128)(2,1)S(1)}, bf16[1,48,3072]{2,1,0:T(8,128)(2,1)S(1)}, u32[]{:S(2)}, u32[]{:S(2)}) collective-permute-start(bf16[1,48,3072]{2,1,0:T(8,128)(2,1)S(1)} %get-tuple-element.239), channel_id=1, source_target_pairs={{0,16},{2,18},{4,20},{6,22},{8,24},{10,26},{12,28},{14,30},{16,0},... | collective-permute-start | bytes 884744 | tf_op jit(solution)/shard_map/rs_ffn_4/ppermute | solution.py:49
  (71 other events, 491.7 us)
Sparse Core Ops, SparseCore 0:
  14.4 85.4 all-gather.1

commit v2 on v1

--- a/solution.py
+++ b/solution.py
@@ -904,14 +904,18 @@
     out_tokens, early_all = taken_out(sent_tokens, block)
     out_grad, late_all = taken_out(sent_grad, block)
     tail.deal()
+    ffn.after(tail.dealt)
+    tail.send()
     ffn.deal()
+    tail.deal()
     tail.dealt, ffn.dealt = lax.optimization_barrier((tail.dealt, ffn.dealt))
     ffn.send()
     tail.send()
+    tail.deal()
+    ffn.after(tail.dealt)
+    tail.send()
     ffn_sum = ffn.finish()
     down_sum, up_sum = ffn_sum[:, :hidden_cols], ffn_sum[:, hidden_cols:]
-    attn_sum = tail.finish()
-    three_sum, back_sum = attn_sum[:, : 3 * head_cols], attn_sum[:, 3 * head_cols :]
 
     (early_sum,) = call(
         functools.partial(gathered_kernel, early_count), [((early_count, width), F32)], (early_all,), "early_sum", 0.5
@@ -931,6 +935,9 @@
         [low_late.reshape(1, 2, head_cols), high_late.reshape(1, 2, head_cols)], axis=2
     )
 
+    tail.after(out_grad)
+    attn_sum = tail.finish()
+    three_sum, back_sum = attn_sum[:, : 3 * head_cols], attn_sum[:, 3 * head_cols :]
     three_out = three_sum.reshape(shard_rows, pairs, 3, PAIR)
     three_out = three_out.transpose(2, 0, 1, 3).reshape(1, 3, shard_rows, head_cols)
     back_out = back_sum.T[None]

time: 298 us -> 295 us (0.990)
  waiting for transfers between devices: 80.4 us -> 75.5 us
  starting transfers between devices: 70.1 us -> 73.5 us
    ppermute x40, waiting for transfers between devices: 78.2 us -> 73.3 us  [xor_permute(): return lax.ppermute(x, axis, [(i, i ^ mask) for i in range(n)])]
    ppermute x40, starting transfers between devices: 42.1 us -> 45.6 us  [xor_permute(): return lax.ppermute(x, axis, [(i, i ^ mask) for i in range(n)])]
  transfers between devices with their start and end apart: 45 -> 45, of which waited for: 24 -> 25; matrix products, arithmetic and copies ran while one was open for 8% -> 8% of each run, Pallas kernels for 26% -> 26%
where the time goes in v2:
time: 295 us; the launch traced here: 291 us
  Pallas kernels  91.5 us (31%)
  waiting for transfers between devices  75.5 us (26%)
  starting transfers between devices  73.5 us (25%)
  local copies, waits for them, and re-layouts  25.5 us (9%)
  between operations  17.2 us (6%)
  other arithmetic  8 us (3%)
    ppermute x40, waiting for transfers between devices, xor_permute(): return lax.ppermute(x, axis, [(i, i ^ mask) for i in range(n)])  73.3 us
    ppermute x40, starting transfers between devices, xor_permute(): return lax.ppermute(x, axis, [(i, i ^ mask) for i in range(n)])  45.6 us
    pallas_call x16, Pallas kernels, call(): pl.pallas_call(kernel, out_shape=[jax.ShapeDtypeStruct(shape, kind) for s...  32.9 us
    pallas_call x2, Pallas kernels, attend_backward(): pl.pallas_call(functools.partial(attend_backward_kernel, min(256, length)...  21.9 us
    pallas_call x3, Pallas kernels, attend_forward(): pl.pallas_call(functools.partial(attend_forward_kernel, min(256, length))...  18 us
    all_to_all x2, starting transfers between devices, exchange_out(): return lax.all_to_all(blocks, 'dp', split_axis=0, concat_axis=0, tiled=True)  16.5 us
    pallas_call x9, Pallas kernels, route(): pl.pallas_call(functools.partial(route_kernel, tuple(plan), kinds, len(ou...  16.4 us
    all_to_all x2, starting transfers between devices, exchange_in(): lax.all_to_all(dealt, 'dp', split_axis=0, concat_axis=0, tiled=True)  11.4 us
  transfers between devices with their start and end apart: 45, of which 25 were waited for; matrix products, arithmetic and copies ran while one was open for 8% of the time, Pallas kernels for 26%

profile of v2, /device:TPU:0, one launch (start us, length us, event | category | flops | bytes accessed | tf_op | source)
XLA Modules:
  0.0 291.2 jit_solution(1541584551814089576)
XLA Ops:
  8.5 5.1 %collective-permute-start.2 = (bf16[1,48,1152]{2,1,0:T(8,128)(2,1)S(1)}, bf16[1,48,1152]{2,1,0:T(8,128)(2,1)S(1)}, u32[]{:S(2)}, u32[]{:S(2)}) collective-permute-start(bf16[1,48,1152]{2,1,0:T(8,128)(2,1)S(1)} %broadcast_in_dim_reshape.3), channel_id=1, source_target_pairs={{0,24},{2,26},{4,28},{6,30},{8,16},{10,18},{12,20},{14,22},{16,8},... | collective-permute-start | bytes 331784 | tf_op jit(solution)/shard_map/ag_three_first/ppermute | solution.py:49
  22.9 5.8 %all-to-all-start = ((bf16[16,32,768]{2,1,0:T(8,128)(2,1)}), bf16[16,32,768]{2,1,0:T(8,128)(2,1)S(1)}, u32[]{:S(2)}, u32[]{:S(2)}) async-start(bf16[16,32,768]{2,1,0:T(8,128)(2,1)} %gather_fusion), calls=%async_computation | async-start | bytes 1572864 | tf_op jit(solution)/shard_map/in_tokens/all_to_all | solution.py:643
  40.1 3.9 %collective-permute-done.5 = bf16[4,48,640]{2,1,0:T(8,128)(2,1)S(1)} collective-permute-done((bf16[4,48,640]{2,1,0:T(8,128)(2,1)S(1)}, bf16[4,48,640]{2,1,0:T(8,128)(2,1)S(1)}, u32[]{:S(2)}, u32[]{:S(2)}) %collective-permute-start.5) | collective-permute-done | bytes 245792 | tf_op jit(solution)/shard_map/ag_three_next/ppermute | solution.py:49
  50.2 5.0 %collective-permute-start.11 = (bf16[1,48,1920]{2,1,0:T(8,128)(2,1)}, bf16[1,48,1920]{2,1,0:T(8,128)(2,1)S(1)}, u32[]{:S(2)}, u32[]{:S(2)}) collective-permute-start(bf16[1,48,1920]{2,1,0:T(8,128)(2,1)} %bitcast.87), channel_id=1, source_target_pairs={{0,24},{2,26},{4,28},{6,30},{8,16},{10,18},{12,20},{14,22},{16,8},... | collective-permute-start | bytes 552968 | tf_op jit(solution)/shard_map/ag_rest_first/ppermute | solution.py:49
  68.1 5.9 %attend_forward.3 = (bf16[1024,384]{1,0:T(8,128)(2,1)S(1)}, f32[3,2,1024]{2,1,0:T(2,128)S(1)}) custom-call(bf16[1024,1152]{1,0:T(8,128)(2,1)S(1)} %project.1.qkv_ref, f32[1024,1]{1,0:T(8,128)S(1)} %fusion.5.bias_ref), custom_call_target="tpu_custom_call" | custom-call | flops 1017750016 | bytes 1000 | tf_op jit(solution)/shard_map/attend_forward/pallas_call | solution.py:380
  78.0 5.9 %attend_forward.4 = (bf16[1024,384]{1,0:T(8,128)(2,1)S(1)}, f32[3,2,1024]{2,1,0:T(2,128)S(1)}) custom-call(bf16[1024,1152]{1,0:T(8,128)(2,1)S(1)} %project.1.qkv_ref, f32[1024,1]{1,0:T(8,128)S(1)} %fusion.5.bias_ref, bf16[1024,384]{1,0:T(8,128)(2,1)S(1)} %get-tuple-element.139.refs_0_, ...), custom_call_target="tpu_custom_call", output_to_operand_aliasing={{0}: (2, {}), {1}: (3, {})} | custom-call | flops 1017750016 | bytes 1000 | tf_op jit(solution)/shard_map/attend_forward/pallas_call | solution.py:380
  83.9 7.8 %collective-permute-done.13 = bf16[4,48,896]{2,1,0:T(8,128)(2,1)S(1)} collective-permute-done((bf16[4,48,896]{2,1,0:T(8,128)(2,1)S(1)}, bf16[4,48,896]{2,1,0:T(8,128)(2,1)S(1)}, u32[]{:S(2)}, u32[]{:S(2)}) %collective-permute-start.13) | collective-permute-done | bytes 344096 | tf_op jit(solution)/shard_map/ag_rest_next/ppermute | solution.py:49
  95.0 6.3 %attend_forward.5 = (bf16[1024,384]{1,0:T(8,128)(2,1)S(1)}, f32[3,2,1024]{2,1,0:T(2,128)S(1)}) custom-call(bf16[1024,1152]{1,0:T(8,128)(2,1)S(1)} %project.1.qkv_ref, f32[1024,1]{1,0:T(8,128)S(1)} %fusion.5.bias_ref, bf16[1024,384]{1,0:T(8,128)(2,1)S(1)} %get-tuple-element.148.refs_0_, ...), custom_call_target="tpu_custom_call", output_to_operand_aliasing={{0}: (2, {}), {1}: (3, {})} | custom-call | flops 1017750016 | bytes 1000 | tf_op jit(solution)/shard_map/attend_forward/pallas_call | solution.py:380
  101.3 5.7 %all-to-all-start.1 = ((bf16[16,32,768]{2,1,0:T(8,128)(2,1)}), bf16[16,32,768]{2,1,0:T(8,128)(2,1)}, u32[]{:S(2)}, u32[]{:S(2)}) async-start(bf16[16,32,768]{2,1,0:T(8,128)(2,1)} %gather_fusion.1), calls=%async_computation.1 | async-start | bytes 1572864 | tf_op jit(solution)/shard_map/in_cot/all_to_all | solution.py:643
  107.0 8.6 %collective-permute-done.15.refs_3_ = bf16[8,48,896]{2,1,0:T(8,128)(2,1)S(1)} collective-permute-done((bf16[8,48,896]{2,1,0:T(8,128)(2,1)S(1)}, bf16[8,48,896]{2,1,0:T(8,128)(2,1)S(1)}, u32[]{:S(2)}, u32[]{:S(2)}) %collective-permute-start.15) | collective-permute-done | bytes 688160 | tf_op jit(solution)/shard_map/ag_rest_last/ppermute | solution.py:49
  123.5 6.1 %middle.1 = (bf16[1024,768]{1,0:T(8,128)(2,1)S(1)}, f32[1024,1]{1,0:T(8,128)S(1)}, bf16[1024,768]{1,0:T(8,128)(2,1)S(1)}, bf16[1024,1536]{1,0:T(8,128)(2,1)S(1)}, bf16[1024,1536]{1,0:T(8,128)(2,1)S(1)}) custom-call(bf16[1024,768]{1,0:T(8,128)(2,1)S(1)} %copy-done.1, bf16[512,768]{1,0:T(8,128)(2,1)S(1)} %attn_part_0.1.p0, ...), custom_call_target="tpu_custom_call" | custom-call | flops 1380000000 | bytes 1000 | tf_op jit(solution)/shard_map/middle/pallas_call | solution.py:470
  140.1 5.5 %outer.1 = (bf16[512,768]{1,0:T(8,128)(2,1)S(1)}, bf16[1024,768]{1,0:T(8,128)(2,1)S(1)}, f32[3,768]{1,0:T(4,128)S(1)}) custom-call(bf16[1024,768]{1,0:T(8,128)(2,1)S(1)} %copy-done.15, bf16[512,768]{1,0:T(8,128)(2,1)} %ffn_part_0.1.p0, bf16[512,768]{1,0:T(8,128)(2,1)} %ffn_part_1.1.p1, bf16[512,768]{1,0:T(8,128)(2,1)} %collective-permute-done.18.p2, ...), custom_call_target="tpu_custom_call" | custom-call | flops 776249984 | bytes 1000 | tf_op jit(solution)/shard_map/outer/pallas_call | solution.py:470
  156.2 3.9 %rs_ffn_deal_11.1 = (bf16[8,48,1536]{2,1,0:T(8,128)(2,1)S(1)}, bf16[8,48,1536]{2,1,0:T(8,128)(2,1)}) custom-call(bf16[1024,768]{1,0:T(8,128)(2,1)S(1)} %copy-done.27, bf16[1024,1536]{1,0:T(8,128)(2,1)S(1)} %get-tuple-element.174.x_ref.refs_1_), custom_call_target="tpu_custom_call" | custom-call | flops 172500000 | bytes 1000 | tf_op jit(solution)/shard_map/rs_ffn_deal_11/pallas_call | solution.py:237
  168.4 9.1 %all-to-all-start.2 = ((bf16[16,48,768]{2,1,0:T(8,128)(2,1)}), bf16[16,48,768]{2,1,0:T(8,128)(2,1)}, u32[]{:S(2)}, u32[]{:S(2)}) async-start(bf16[16,48,768]{2,1,0:T(8,128)(2,1)} %pad_maximum_fusion.1), calls=%async_computation.2 | async-start | bytes 2359296 | tf_op jit(solution)/shard_map/out_rows/all_to_all | solution.py:652
  178.7 14.7 %attend_backward.2 = (bf16[1024,1152]{1,0:T(8,128)(2,1)S(1)}, f32[3,2,128]{2,1,0:T(2,128)S(1)}) custom-call(bf16[1024,1152]{1,0:T(8,128)(2,1)S(1)} %copy-done.11, bf16[1024,384]{1,0:T(8,128)(2,1)S(1)} %copy-done.33, f32[3,2,1024]{2,1,0:T(2,128)S(1)} %copy-done.38, f32[1024,1]{1,0:T(8,128)S(1)} %copy-done.21), custom_call_target="tpu_custom_call" | custom-call | flops 2518500096 | bytes 1000 | tf_op jit(solution)/shard_map/attend_backward/pallas_call | solution.py:442
  203.3 7.2 %attend_backward.3 = (bf16[1024,1152]{1,0:T(8,128)(2,1)S(1)}, f32[3,2,128]{2,1,0:T(2,128)S(1)}) custom-call(bf16[1024,1152]{1,0:T(8,128)(2,1)S(1)} %copy-done.11, bf16[1024,384]{1,0:T(8,128)(2,1)S(1)} %copy-done.33, f32[3,2,1024]{2,1,0:T(2,128)S(1)} %copy-done.38, f32[1024,1]{1,0:T(8,128)S(1)} %copy-done.21, ...), custom_call_target="tpu_custom_call", output_to_operand_aliasing={{0}: (4, {}), {1}: (5, {})} | custom-call | flops 1259250048 | bytes 1000 | tf_op jit(solution)/shard_map/attend_backward/pallas_call | solution.py:442
  210.5 4.4 %collective-permute-done.26.refs_1_ = bf16[4,48,1536]{2,1,0:T(8,128)(2,1)S(1)} collective-permute-done((bf16[4,48,1536]{2,1,0:T(8,128)(2,1)S(1)}, bf16[4,48,1536]{2,1,0:T(8,128)(2,1)S(1)}, u32[]{:S(2)}, u32[]{:S(2)}) %collective-permute-start.26) | collective-permute-done | bytes 589856 | tf_op jit(solution)/shard_map/rs_ffn_2/ppermute | solution.py:49
  217.2 4.4 %rs_attn_deal_1.1 = (bf16[8,48,768]{2,1,0:T(8,128)(2,1)S(1)}, bf16[8,48,768]{2,1,0:T(8,128)(2,1)}, bf16[8,48,768]{2,1,0:T(8,128)(2,1)S(1)}, bf16[8,48,768]{2,1,0:T(8,128)(2,1)}) custom-call(bf16[1024,768]{1,0:T(8,128)(2,1)S(1)} %copy-done.2, bf16[1024,1152]{1,0:T(8,128)(2,1)S(1)} %get-tuple-element.213.refs_1_.x_ref, bf16[1024,768]{1,0:T(8,128)(2,1)S(1)} %copy-done.25, ...), custom_call_target="tpu_custom_call" | custom-call | flops 172500000 | bytes 1000 | tf_op jit(solution)/shard_map/rs_attn_deal_1/pallas_call | solution.py:237
  228.2 7.4 %all-to-all-start.3 = ((bf16[16,40,768]{2,1,0:T(8,128)(2,1)}), bf16[16,40,768]{2,1,0:T(8,128)(2,1)}, u32[]{:S(2)}, u32[]{:S(2)}) async-start(bf16[16,40,768]{2,1,0:T(8,128)(2,1)} %pad_maximum_fusion.2), calls=%async_computation.3 | async-start | bytes 1966080 | tf_op jit(solution)/shard_map/out_rows/all_to_all | solution.py:652
  240.9 4.4 %collective-permute-done.31.refs_3_ = bf16[8,48,768]{2,1,0:T(8,128)(2,1)S(1)} collective-permute-done((bf16[8,48,768]{2,1,0:T(8,128)(2,1)}, bf16[8,48,768]{2,1,0:T(8,128)(2,1)S(1)}, u32[]{:S(2)}, u32[]{:S(2)}) %collective-permute-start.31) | collective-permute-done | bytes 589856 | tf_op jit(solution)/shard_map/rs_attn_1/ppermute | solution.py:49
  249.7 6.5 %collective-permute-done.32.refs_1_ = bf16[4,48,768]{2,1,0:T(8,128)(2,1)S(1)} collective-permute-done((bf16[4,48,768]{2,1,0:T(8,128)(2,1)S(1)}, bf16[4,48,768]{2,1,0:T(8,128)(2,1)S(1)}, u32[]{:S(2)}, u32[]{:S(2)}) %collective-permute-start.32) | collective-permute-done | bytes 294944 | tf_op jit(solution)/shard_map/rs_attn_2/ppermute | solution.py:49
  259.9 4.9 %collective-permute-start.37 = (bf16[1,48,3072]{2,1,0:T(8,128)(2,1)S(1)}, bf16[1,48,3072]{2,1,0:T(8,128)(2,1)S(1)}, u32[]{:S(2)}, u32[]{:S(2)}) collective-permute-start(bf16[1,48,3072]{2,1,0:T(8,128)(2,1)S(1)} %get-tuple-element.240), channel_id=1, source_target_pairs={{0,16},{2,18},{4,20},{6,22},{8,24},{10,26},{12,28},{14,30},{16,0},... | collective-permute-start | bytes 884744 | tf_op jit(solution)/shard_map/rs_ffn_4/ppermute | solution.py:49
  267.3 4.2 %collective-permute-start.36 = (bf16[1,48,1536]{2,1,0:T(8,128)(2,1)S(1)}, bf16[1,48,1536]{2,1,0:T(8,128)(2,1)S(1)}, u32[]{:S(2)}, u32[]{:S(2)}) collective-permute-start(bf16[1,48,1536]{2,1,0:T(8,128)(2,1)S(1)} %get-tuple-element.237), channel_id=1, source_target_pairs={{0,16},{2,18},{4,20},{6,22},{8,24},{10,26},{12,28},{14,30},{16,0},... | collective-permute-start | bytes 442376 | tf_op jit(solution)/shard_map/rs_attn_4/ppermute | solution.py:49
  271.5 5.5 %collective-permute-done.37 = bf16[1,48,3072]{2,1,0:T(8,128)(2,1)S(1)} collective-permute-done((bf16[1,48,3072]{2,1,0:T(8,128)(2,1)S(1)}, bf16[1,48,3072]{2,1,0:T(8,128)(2,1)S(1)}, u32[]{:S(2)}, u32[]{:S(2)}) %collective-permute-start.37) | collective-permute-done | bytes 294944 | tf_op jit(solution)/shard_map/rs_ffn_4/ppermute | solution.py:49
  (269 shorter events, 125.9 us)
Async XLA Ops:
  7.2 111.5 %all-gather.2.cloned.1.call-start = ((), (), s32[]{:S(2)}) async-start(), calls=%async_computation.4 | async-start | bytes 2506752 | tf_op jit(solution)/shard_map/all_gather | solution.py:741
  8.5 14.5 %collective-permute-start.2 = (bf16[1,48,1152]{2,1,0:T(8,128)(2,1)S(1)}, bf16[1,48,1152]{2,1,0:T(8,128)(2,1)S(1)}, u32[]{:S(2)}, u32[]{:S(2)}) collective-permute-start(bf16[1,48,1152]{2,1,0:T(8,128)(2,1)S(1)} %broadcast_in_dim_reshape.3), channel_id=1, source_target_pairs={{0,24},{2,26},{4,28},{6,30},{8,16},{10,18},{12,20},{14,22},{16,8},... | collective-permute-start | bytes 331784 | tf_op jit(solution)/shard_map/ag_three_first/ppermute | solution.py:49
  22.9 26.6 %all-to-all-start = ((bf16[16,32,768]{2,1,0:T(8,128)(2,1)}), bf16[16,32,768]{2,1,0:T(8,128)(2,1)S(1)}, u32[]{:S(2)}, u32[]{:S(2)}) async-start(bf16[16,32,768]{2,1,0:T(8,128)(2,1)} %gather_fusion), calls=%async_computation | async-start | bytes 1572864 | tf_op jit(solution)/shard_map/in_tokens/all_to_all | solution.py:643
  47.0 15.6 %collective-permute-start.7 = (bf16[8,48,640]{2,1,0:T(8,128)(2,1)S(1)}, bf16[8,48,640]{2,1,0:T(8,128)(2,1)S(1)}, u32[]{:S(2)}, u32[]{:S(2)}) collective-permute-start(bf16[8,48,640]{2,1,0:T(8,128)(2,1)S(1)} %pad_maximum_fusion.6.refs_0_), channel_id=1, source_target_pairs={{0,2},{2,0},{4,6},{6,4},{8,10},{10,8},{12,14},{14,12},{16,18},{18,... | collective-permute-start | bytes 1474568 | tf_op jit(solution)/shard_map/ag_three_last/ppermute | solution.py:49
  49.6 14.7 %collective-permute-start.4 = (bf16[256,768]{1,0:T(8,128)(2,1)S(1)}, bf16[256,768]{1,0:T(8,128)(2,1)S(1)}, u32[]{:S(2)}, u32[]{:S(2)}) collective-permute-start(bf16[256,768]{1,0:T(8,128)(2,1)S(1)} %bitcast.93), channel_id=1, source_target_pairs={{0,1},{1,0},{2,3},{3,2},{4,5},{5,4},{6,7},{7,6},{8,9},{9,8},{10,11... | collective-permute-start | bytes 1179656 | tf_op jit(solution)/shard_map/ppermute | solution.py:49
  49.6 14.6 %collective-permute-start.3 = (bf16[256,768]{1,0:T(8,128)(2,1)S(1)}, bf16[256,768]{1,0:T(8,128)(2,1)S(1)}, u32[]{:S(2)}, u32[]{:S(2)}) collective-permute-start(bf16[256,768]{1,0:T(8,128)(2,1)S(1)} %bitcast.92), channel_id=1, source_target_pairs={{0,1},{1,0},{2,3},{3,2},{4,5},{5,4},{6,7},{7,6},{8,9},{9,8},{10,11... | collective-permute-start | bytes 1179656 | tf_op jit(solution)/shard_map/ppermute | solution.py:49
  50.2 23.8 %collective-permute-start.11 = (bf16[1,48,1920]{2,1,0:T(8,128)(2,1)}, bf16[1,48,1920]{2,1,0:T(8,128)(2,1)S(1)}, u32[]{:S(2)}, u32[]{:S(2)}) collective-permute-start(bf16[1,48,1920]{2,1,0:T(8,128)(2,1)} %bitcast.87), channel_id=1, source_target_pairs={{0,24},{2,26},{4,28},{6,30},{8,16},{10,18},{12,20},{14,22},{16,8},... | collective-permute-start | bytes 552968 | tf_op jit(solution)/shard_map/ag_rest_first/ppermute | solution.py:49
  57.8 17.0 %collective-permute-start.10 = (bf16[1,48,1920]{2,1,0:T(8,128)(2,1)}, bf16[1,48,1920]{2,1,0:T(8,128)(2,1)S(1)}, u32[]{:S(2)}, u32[]{:S(2)}) collective-permute-start(bf16[1,48,1920]{2,1,0:T(8,128)(2,1)} %bitcast.88), channel_id=1, source_target_pairs={{0,16},{2,18},{4,20},{6,22},{8,24},{10,26},{12,28},{14,30},{16,0},... | collective-permute-start | bytes 552968 | tf_op jit(solution)/shard_map/ag_rest_first/ppermute | solution.py:49
  74.9 17.8 %collective-permute-start.12 = (bf16[4,48,1024]{2,1,0:T(8,128)(2,1)S(1)}, bf16[4,48,1024]{2,1,0:T(8,128)(2,1)S(1)}, u32[]{:S(2)}, u32[]{:S(2)}) collective-permute-start(bf16[4,48,1024]{2,1,0:T(8,128)(2,1)S(1)} %slice.124), channel_id=1, source_target_pairs={{0,4},{2,6},{4,0},{6,2},{8,12},{10,14},{12,8},{14,10},{16,20},{18,... | collective-permute-start | bytes 1179656 | tf_op jit(solution)/shard_map/ag_rest_next/ppermute | solution.py:49
  77.2 14.5 %collective-permute-start.13 = (bf16[4,48,896]{2,1,0:T(8,128)(2,1)S(1)}, bf16[4,48,896]{2,1,0:T(8,128)(2,1)S(1)}, u32[]{:S(2)}, u32[]{:S(2)}) collective-permute-start(bf16[4,48,896]{2,1,0:T(8,128)(2,1)S(1)} %slice.125), channel_id=1, source_target_pairs={{0,2},{2,0},{4,6},{6,4},{8,10},{10,8},{12,14},{14,12},{16,18},{18,... | collective-permute-start | bytes 1032200 | tf_op jit(solution)/shard_map/ag_rest_next/ppermute | solution.py:49
  92.9 22.7 %collective-permute-start.14 = (bf16[8,48,1024]{2,1,0:T(8,128)(2,1)S(1)}, bf16[8,48,1024]{2,1,0:T(8,128)(2,1)}, u32[]{:S(2)}, u32[]{:S(2)}) collective-permute-start(bf16[8,48,1024]{2,1,0:T(8,128)(2,1)S(1)} %pad_maximum_fusion.3.refs_0_), channel_id=1, source_target_pairs={{0,2},{2,0},{4,6},{6,4},{8,10},{10,8},{12,14},{14,12},{16,18},{18,... | collective-permute-start | bytes 2359304 | tf_op jit(solution)/shard_map/ag_rest_last/ppermute | solution.py:49
  94.4 21.1 %collective-permute-start.15 = (bf16[8,48,896]{2,1,0:T(8,128)(2,1)S(1)}, bf16[8,48,896]{2,1,0:T(8,128)(2,1)S(1)}, u32[]{:S(2)}, u32[]{:S(2)}) collective-permute-start(bf16[8,48,896]{2,1,0:T(8,128)(2,1)S(1)} %pad_maximum_fusion.5.refs_2_), channel_id=1, source_target_pairs={{0,4},{2,6},{4,0},{6,2},{8,12},{10,14},{12,8},{14,10},{16,20},{18,... | collective-permute-start | bytes 2064392 | tf_op jit(solution)/shard_map/ag_rest_last/ppermute | solution.py:49
  101.3 34.7 %all-to-all-start.1 = ((bf16[16,32,768]{2,1,0:T(8,128)(2,1)}), bf16[16,32,768]{2,1,0:T(8,128)(2,1)}, u32[]{:S(2)}, u32[]{:S(2)}) async-start(bf16[16,32,768]{2,1,0:T(8,128)(2,1)} %gather_fusion.1), calls=%async_computation.1 | async-start | bytes 1572864 | tf_op jit(solution)/shard_map/in_cot/all_to_all | solution.py:643
  156.2 37.1 %collective-permute-start.24 = (bf16[8,48,1536]{2,1,0:T(8,128)(2,1)}, bf16[8,48,1536]{2,1,0:T(8,128)(2,1)}, u32[]{:S(2)}, u32[]{:S(2)}) collective-permute-start(bf16[8,48,1536]{2,1,0:T(8,128)(2,1)} %get-tuple-element.184), channel_id=1, source_target_pairs={{0,2},{2,0},{4,6},{6,4},{8,10},{10,8},{12,14},{14,12},{16,18},{18,... | collective-permute-start | bytes 3538952 | tf_op jit(solution)/shard_map/rs_ffn_10/ppermute | solution.py:49
  160.2 37.0 %collective-permute-start.25 = (bf16[8,48,1536]{2,1,0:T(8,128)(2,1)}, bf16[8,48,1536]{2,1,0:T(8,128)(2,1)}, u32[]{:S(2)}, u32[]{:S(2)}) collective-permute-start(bf16[8,48,1536]{2,1,0:T(8,128)(2,1)} %get-tuple-element.185), channel_id=1, source_target_pairs={{0,4},{2,6},{4,0},{6,2},{8,12},{10,14},{12,8},{14,10},{16,20},{18,... | collective-permute-start | bytes 3538952 | tf_op jit(solution)/shard_map/rs_ffn_11/ppermute | solution.py:49
  168.4 59.8 %all-to-all-start.2 = ((bf16[16,48,768]{2,1,0:T(8,128)(2,1)}), bf16[16,48,768]{2,1,0:T(8,128)(2,1)}, u32[]{:S(2)}, u32[]{:S(2)}) async-start(bf16[16,48,768]{2,1,0:T(8,128)(2,1)} %pad_maximum_fusion.1), calls=%async_computation.2 | async-start | bytes 2359296 | tf_op jit(solution)/shard_map/out_rows/all_to_all | solution.py:652
  199.7 15.3 %collective-permute-start.26 = (bf16[4,48,1536]{2,1,0:T(8,128)(2,1)S(1)}, bf16[4,48,1536]{2,1,0:T(8,128)(2,1)S(1)}, u32[]{:S(2)}, u32[]{:S(2)}) collective-permute-start(bf16[4,48,1536]{2,1,0:T(8,128)(2,1)S(1)} %get-tuple-element.199), channel_id=1, source_target_pairs={{0,4},{2,6},{4,0},{6,2},{8,12},{10,14},{12,8},{14,10},{16,20},{18,... | collective-permute-start | bytes 1769480 | tf_op jit(solution)/shard_map/rs_ffn_2/ppermute | solution.py:49
  201.6 14.5 %collective-permute-start.27 = (bf16[4,48,1536]{2,1,0:T(8,128)(2,1)S(1)}, bf16[4,48,1536]{2,1,0:T(8,128)(2,1)S(1)}, u32[]{:S(2)}, u32[]{:S(2)}) collective-permute-start(bf16[4,48,1536]{2,1,0:T(8,128)(2,1)S(1)} %get-tuple-element.200), channel_id=1, source_target_pairs={{0,2},{2,0},{4,6},{6,4},{8,10},{10,8},{12,14},{14,12},{16,18},{18,... | collective-permute-start | bytes 1769480 | tf_op jit(solution)/shard_map/rs_ffn_2/ppermute | solution.py:49
  224.5 16.4 %collective-permute-start.30 = (bf16[8,48,768]{2,1,0:T(8,128)(2,1)}, bf16[8,48,768]{2,1,0:T(8,128)(2,1)S(1)}, u32[]{:S(2)}, u32[]{:S(2)}) collective-permute-start(bf16[8,48,768]{2,1,0:T(8,128)(2,1)} %get-tuple-element.220), channel_id=1, source_target_pairs={{0,2},{2,0},{4,6},{6,4},{8,10},{10,8},{12,14},{14,12},{16,18},{18,... | collective-permute-start | bytes 1769480 | tf_op jit(solution)/shard_map/rs_attn_1/ppermute | solution.py:49
  225.6 19.7 %collective-permute-start.31 = (bf16[8,48,768]{2,1,0:T(8,128)(2,1)}, bf16[8,48,768]{2,1,0:T(8,128)(2,1)S(1)}, u32[]{:S(2)}, u32[]{:S(2)}) collective-permute-start(bf16[8,48,768]{2,1,0:T(8,128)(2,1)} %get-tuple-element.222), channel_id=1, source_target_pairs={{0,4},{2,6},{4,0},{6,2},{8,12},{10,14},{12,8},{14,10},{16,20},{18,... | collective-permute-start | bytes 1769480 | tf_op jit(solution)/shard_map/rs_attn_1/ppermute | solution.py:49
  226.5 23.0 %collective-permute-start.34 = (bf16[2,48,3072]{2,1,0:T(8,128)(2,1)}, bf16[2,48,3072]{2,1,0:T(8,128)(2,1)S(1)}, u32[]{:S(2)}, u32[]{:S(2)}) collective-permute-start(bf16[2,48,3072]{2,1,0:T(8,128)(2,1)} %get-tuple-element.230), channel_id=1, source_target_pairs={{0,8},{2,10},{4,12},{6,14},{8,0},{10,2},{12,4},{14,6},{16,24},{18,... | collective-permute-start | bytes 1769480 | tf_op jit(solution)/shard_map/rs_ffn_3/ppermute | solution.py:49
  228.2 49.8 %all-to-all-start.3 = ((bf16[16,40,768]{2,1,0:T(8,128)(2,1)}), bf16[16,40,768]{2,1,0:T(8,128)(2,1)}, u32[]{:S(2)}, u32[]{:S(2)}) async-start(bf16[16,40,768]{2,1,0:T(8,128)(2,1)} %pad_maximum_fusion.2), calls=%async_computation.3 | async-start | bytes 1966080 | tf_op jit(solution)/shard_map/out_rows/all_to_all | solution.py:652
  245.8 13.9 %collective-permute-start.33 = (bf16[4,48,768]{2,1,0:T(8,128)(2,1)S(1)}, bf16[4,48,768]{2,1,0:T(8,128)(2,1)S(1)}, u32[]{:S(2)}, u32[]{:S(2)}) collective-permute-start(bf16[4,48,768]{2,1,0:T(8,128)(2,1)S(1)} %get-tuple-element.226), channel_id=1, source_target_pairs={{0,2},{2,0},{4,6},{6,4},{8,10},{10,8},{12,14},{14,12},{16,18},{18,... | collective-permute-start | bytes 884744 | tf_op jit(solution)/shard_map/rs_attn_2/ppermute | solution.py:49
  259.9 17.1 %collective-permute-start.37 = (bf16[1,48,3072]{2,1,0:T(8,128)(2,1)S(1)}, bf16[1,48,3072]{2,1,0:T(8,128)(2,1)S(1)}, u32[]{:S(2)}, u32[]{:S(2)}) collective-permute-start(bf16[1,48,3072]{2,1,0:T(8,128)(2,1)S(1)} %get-tuple-element.240), channel_id=1, source_target_pairs={{0,16},{2,18},{4,20},{6,22},{8,24},{10,26},{12,28},{14,30},{16,0},... | collective-permute-start | bytes 884744 | tf_op jit(solution)/shard_map/rs_ffn_4/ppermute | solution.py:49
  (71 other events, 499.6 us)
Sparse Core Ops, SparseCore 0:
  14.4 85.4 all-gather.1

commit v3 on v2

--- a/solution.py
+++ b/solution.py
@@ -378,7 +378,7 @@
 def attend_forward(qkv, bias, first, pairs, total, known=()):
     length = qkv.shape[0]
     return pl.pallas_call(
-        functools.partial(attend_forward_kernel, min(256, length)),
+        functools.partial(attend_forward_kernel, min(512, length)),
         grid=(pairs,),
         out_shape=(
             jax.ShapeDtypeStruct((length, total * PAIR), BF16),
@@ -394,7 +394,7 @@
             pl.BlockSpec((1, 2, length), lambda p: (p + first, 0, 0)),
         ),
         input_output_aliases={2: 0, 3: 1} if known else {},
-        compiler_params=pltpu.CompilerParams(vmem_limit_bytes=10 << 20),
+        compiler_params=pltpu.CompilerParams(vmem_limit_bytes=16 << 20),
         cost_estimate=cost(5.9 * pairs),
         name="attend_forward",
     )(qkv, bias, *known)
@@ -459,7 +459,7 @@
         ),
         input_output_aliases={4: 0, 5: 1} if known else {},
         scratch_shapes=[pltpu.VMEM((length, HEAD_DIM), F32), pltpu.VMEM((length, HEAD_DIM), F32)],
-        compiler_params=pltpu.CompilerParams(vmem_limit_bytes=10 << 20),
+        compiler_params=pltpu.CompilerParams(vmem_limit_bytes=16 << 20),
         cost_estimate=cost(7.3 * pairs),
         name="attend_backward",
     )(qkv, dctx, lse, bias, *known)

time: 295 us -> 299 us (1.014)
  waiting for transfers between devices: 75.5 us -> 90.1 us
  Pallas kernels: 91.5 us -> 86.5 us
  starting transfers between devices: 73.5 us -> 68.7 us
    ppermute x40, waiting for transfers between devices: 73.3 us -> 87.9 us  [xor_permute(): return lax.ppermute(x, axis, [(i, i ^ mask) for i in range(n)])]
    pallas_call x3, Pallas kernels: 18 us -> 12.4 us  [attend_forward(): pl.pallas_call(functools.partial(attend_forward_kernel, min(512, length))...]
  transfers between devices with their start and end apart: 45 -> 45, of which waited for: 25 -> 26; matrix products, arithmetic and copies ran while one was open for 8% -> 8% of each run, Pallas kernels for 26% -> 24%
where the time goes in v3:
time: 299 us; the launch traced here: 296 us
  waiting for transfers between devices  90.1 us (30%)
  Pallas kernels  86.5 us (29%)
  starting transfers between devices  68.7 us (23%)
  local copies, waits for them, and re-layouts  25.5 us (9%)
  between operations  17.1 us (6%)
  other arithmetic  8 us (3%)
    ppermute x40, waiting for transfers between devices, xor_permute(): return lax.ppermute(x, axis, [(i, i ^ mask) for i in range(n)])  87.9 us
    ppermute x40, starting transfers between devices, xor_permute(): return lax.ppermute(x, axis, [(i, i ^ mask) for i in range(n)])  43.1 us
    pallas_call x16, Pallas kernels, call(): pl.pallas_call(kernel, out_shape=[jax.ShapeDtypeStruct(shape, kind) for s...  33.3 us
    pallas_call x2, Pallas kernels, attend_backward(): pl.pallas_call(functools.partial(attend_backward_kernel, min(256, length)...  21.9 us
    pallas_call x9, Pallas kernels, route(): pl.pallas_call(functools.partial(route_kernel, tuple(plan), kinds, len(ou...  16.6 us
    all_to_all x2, starting transfers between devices, exchange_out(): return lax.all_to_all(blocks, 'dp', split_axis=0, concat_axis=0, tiled=True)  14 us
    pallas_call x3, Pallas kernels, attend_forward(): pl.pallas_call(functools.partial(attend_forward_kernel, min(512, length))...  12.4 us
    all_to_all x2, starting transfers between devices, exchange_in(): lax.all_to_all(dealt, 'dp', split_axis=0, concat_axis=0, tiled=True)  11.6 us
  transfers between devices with their start and end apart: 45, of which 26 were waited for; matrix products, arithmetic and copies ran while one was open for 8% of the time, Pallas kernels for 24%

profile of v3, /device:TPU:0, one launch (start us, length us, event | category | flops | bytes accessed | tf_op | source)
XLA Modules:
  0.0 295.9 jit_solution(1524392943998677169)
XLA Ops:
  8.5 5.1 %collective-permute-start.2 = (bf16[1,48,1152]{2,1,0:T(8,128)(2,1)S(1)}, bf16[1,48,1152]{2,1,0:T(8,128)(2,1)S(1)}, u32[]{:S(2)}, u32[]{:S(2)}) collective-permute-start(bf16[1,48,1152]{2,1,0:T(8,128)(2,1)S(1)} %broadcast_in_dim_reshape.3), channel_id=1, source_target_pairs={{0,24},{2,26},{4,28},{6,30},{8,16},{10,18},{12,20},{14,22},{16,8},... | collective-permute-start | bytes 331784 | tf_op jit(solution)/shard_map/ag_three_first/ppermute | solution.py:49
  22.9 5.8 %all-to-all-start = ((bf16[16,32,768]{2,1,0:T(8,128)(2,1)}), bf16[16,32,768]{2,1,0:T(8,128)(2,1)S(1)}, u32[]{:S(2)}, u32[]{:S(2)}) async-start(bf16[16,32,768]{2,1,0:T(8,128)(2,1)} %gather_fusion), calls=%async_computation | async-start | bytes 1572864 | tf_op jit(solution)/shard_map/in_tokens/all_to_all | solution.py:643
  40.1 3.9 %collective-permute-done.5 = bf16[4,48,640]{2,1,0:T(8,128)(2,1)S(1)} collective-permute-done((bf16[4,48,640]{2,1,0:T(8,128)(2,1)S(1)}, bf16[4,48,640]{2,1,0:T(8,128)(2,1)S(1)}, u32[]{:S(2)}, u32[]{:S(2)}) %collective-permute-start.5) | collective-permute-done | bytes 245792 | tf_op jit(solution)/shard_map/ag_three_next/ppermute | solution.py:49
  50.2 5.0 %collective-permute-start.11 = (bf16[1,48,1920]{2,1,0:T(8,128)(2,1)}, bf16[1,48,1920]{2,1,0:T(8,128)(2,1)S(1)}, u32[]{:S(2)}, u32[]{:S(2)}) collective-permute-start(bf16[1,48,1920]{2,1,0:T(8,128)(2,1)} %bitcast.87), channel_id=1, source_target_pairs={{0,24},{2,26},{4,28},{6,30},{8,16},{10,18},{12,20},{14,22},{16,8},... | collective-permute-start | bytes 552968 | tf_op jit(solution)/shard_map/ag_rest_first/ppermute | solution.py:49
  68.5 4.1 %attend_forward.3 = (bf16[1024,384]{1,0:T(8,128)(2,1)S(1)}, f32[3,2,1024]{2,1,0:T(2,128)S(1)}) custom-call(bf16[1024,1152]{1,0:T(8,128)(2,1)S(1)} %project.1.qkv_ref, f32[1024,1]{1,0:T(8,128)S(1)} %fusion.5.bias_ref), custom_call_target="tpu_custom_call" | custom-call | flops 1017750016 | bytes 1000 | tf_op jit(solution)/shard_map/attend_forward/pallas_call | solution.py:380
  78.0 4.1 %attend_forward.4 = (bf16[1024,384]{1,0:T(8,128)(2,1)S(1)}, f32[3,2,1024]{2,1,0:T(2,128)S(1)}) custom-call(bf16[1024,1152]{1,0:T(8,128)(2,1)S(1)} %project.1.qkv_ref, f32[1024,1]{1,0:T(8,128)S(1)} %fusion.5.bias_ref, bf16[1024,384]{1,0:T(8,128)(2,1)S(1)} %get-tuple-element.139.refs_0_, ...), custom_call_target="tpu_custom_call", output_to_operand_aliasing={{0}: (2, {}), {1}: (3, {})} | custom-call | flops 1017750016 | bytes 1000 | tf_op jit(solution)/shard_map/attend_forward/pallas_call | solution.py:380
  82.2 9.5 %collective-permute-done.13 = bf16[4,48,896]{2,1,0:T(8,128)(2,1)S(1)} collective-permute-done((bf16[4,48,896]{2,1,0:T(8,128)(2,1)S(1)}, bf16[4,48,896]{2,1,0:T(8,128)(2,1)S(1)}, u32[]{:S(2)}, u32[]{:S(2)}) %collective-permute-start.13) | collective-permute-done | bytes 344096 | tf_op jit(solution)/shard_map/ag_rest_next/ppermute | solution.py:49
  95.0 4.1 %attend_forward.5 = (bf16[1024,384]{1,0:T(8,128)(2,1)S(1)}, f32[3,2,1024]{2,1,0:T(2,128)S(1)}) custom-call(bf16[1024,1152]{1,0:T(8,128)(2,1)S(1)} %project.1.qkv_ref, f32[1024,1]{1,0:T(8,128)S(1)} %fusion.5.bias_ref, bf16[1024,384]{1,0:T(8,128)(2,1)S(1)} %get-tuple-element.148.refs_0_, ...), custom_call_target="tpu_custom_call", output_to_operand_aliasing={{0}: (2, {}), {1}: (3, {})} | custom-call | flops 1017750016 | bytes 1000 | tf_op jit(solution)/shard_map/attend_forward/pallas_call | solution.py:380
  99.2 5.9 %all-to-all-start.1 = ((bf16[16,32,768]{2,1,0:T(8,128)(2,1)}), bf16[16,32,768]{2,1,0:T(8,128)(2,1)}, u32[]{:S(2)}, u32[]{:S(2)}) async-start(bf16[16,32,768]{2,1,0:T(8,128)(2,1)} %gather_fusion.1), calls=%async_computation.1 | async-start | bytes 1572864 | tf_op jit(solution)/shard_map/in_cot/all_to_all | solution.py:643
  105.0 11.5 %collective-permute-done.15.refs_3_ = bf16[8,48,896]{2,1,0:T(8,128)(2,1)S(1)} collective-permute-done((bf16[8,48,896]{2,1,0:T(8,128)(2,1)S(1)}, bf16[8,48,896]{2,1,0:T(8,128)(2,1)S(1)}, u32[]{:S(2)}, u32[]{:S(2)}) %collective-permute-start.15) | collective-permute-done | bytes 688160 | tf_op jit(solution)/shard_map/ag_rest_last/ppermute | solution.py:49
  124.4 6.1 %middle.1 = (bf16[1024,768]{1,0:T(8,128)(2,1)S(1)}, f32[1024,1]{1,0:T(8,128)S(1)}, bf16[1024,768]{1,0:T(8,128)(2,1)S(1)}, bf16[1024,1536]{1,0:T(8,128)(2,1)S(1)}, bf16[1024,1536]{1,0:T(8,128)(2,1)S(1)}) custom-call(bf16[1024,768]{1,0:T(8,128)(2,1)S(1)} %copy-done.1, bf16[512,768]{1,0:T(8,128)(2,1)S(1)} %attn_part_0.1.p0, ...), custom_call_target="tpu_custom_call" | custom-call | flops 1380000000 | bytes 1000 | tf_op jit(solution)/shard_map/middle/pallas_call | solution.py:470
  141.0 5.5 %outer.1 = (bf16[512,768]{1,0:T(8,128)(2,1)S(1)}, bf16[1024,768]{1,0:T(8,128)(2,1)S(1)}, f32[3,768]{1,0:T(4,128)S(1)}) custom-call(bf16[1024,768]{1,0:T(8,128)(2,1)S(1)} %copy-done.15, bf16[512,768]{1,0:T(8,128)(2,1)} %ffn_part_0.1.p0, bf16[512,768]{1,0:T(8,128)(2,1)} %ffn_part_1.1.p1, bf16[512,768]{1,0:T(8,128)(2,1)} %collective-permute-done.18.p2, ...), custom_call_target="tpu_custom_call" | custom-call | flops 776249984 | bytes 1000 | tf_op jit(solution)/shard_map/outer/pallas_call | solution.py:470
  158.8 3.9 %rs_ffn_deal_11.1 = (bf16[8,48,1536]{2,1,0:T(8,128)(2,1)S(1)}, bf16[8,48,1536]{2,1,0:T(8,128)(2,1)}) custom-call(bf16[1024,768]{1,0:T(8,128)(2,1)S(1)} %copy-done.27, bf16[1024,1536]{1,0:T(8,128)(2,1)S(1)} %get-tuple-element.174.x_ref.refs_1_), custom_call_target="tpu_custom_call" | custom-call | flops 172500000 | bytes 1000 | tf_op jit(solution)/shard_map/rs_ffn_deal_11/pallas_call | solution.py:237
  171.0 7.0 %all-to-all-start.2 = ((bf16[16,48,768]{2,1,0:T(8,128)(2,1)}), bf16[16,48,768]{2,1,0:T(8,128)(2,1)}, u32[]{:S(2)}, u32[]{:S(2)}) async-start(bf16[16,48,768]{2,1,0:T(8,128)(2,1)} %pad_maximum_fusion.1), calls=%async_computation.2 | async-start | bytes 2359296 | tf_op jit(solution)/shard_map/out_rows/all_to_all | solution.py:652
  179.1 14.7 %attend_backward.2 = (bf16[1024,1152]{1,0:T(8,128)(2,1)S(1)}, f32[3,2,128]{2,1,0:T(2,128)S(1)}) custom-call(bf16[1024,1152]{1,0:T(8,128)(2,1)S(1)} %copy-done.11, bf16[1024,384]{1,0:T(8,128)(2,1)S(1)} %copy-done.33, f32[3,2,1024]{2,1,0:T(2,128)S(1)} %copy-done.38, f32[1024,1]{1,0:T(8,128)S(1)} %copy-done.21), custom_call_target="tpu_custom_call" | custom-call | flops 2518500096 | bytes 1000 | tf_op jit(solution)/shard_map/attend_backward/pallas_call | solution.py:442
  193.8 7.0 %collective-permute-done.25.refs_3_ = bf16[8,48,1536]{2,1,0:T(8,128)(2,1)} collective-permute-done((bf16[8,48,1536]{2,1,0:T(8,128)(2,1)}, bf16[8,48,1536]{2,1,0:T(8,128)(2,1)}, u32[]{:S(2)}, u32[]{:S(2)}) %collective-permute-start.25) | collective-permute-done | bytes 1179680 | tf_op jit(solution)/shard_map/rs_ffn_11/ppermute | solution.py:49
  204.5 7.2 %attend_backward.3 = (bf16[1024,1152]{1,0:T(8,128)(2,1)S(1)}, f32[3,2,128]{2,1,0:T(2,128)S(1)}) custom-call(bf16[1024,1152]{1,0:T(8,128)(2,1)S(1)} %copy-done.11, bf16[1024,384]{1,0:T(8,128)(2,1)S(1)} %copy-done.33, f32[3,2,1024]{2,1,0:T(2,128)S(1)} %copy-done.38, f32[1024,1]{1,0:T(8,128)S(1)} %copy-done.21, ...), custom_call_target="tpu_custom_call", output_to_operand_aliasing={{0}: (4, {}), {1}: (5, {})} | custom-call | flops 1259250048 | bytes 1000 | tf_op jit(solution)/shard_map/attend_backward/pallas_call | solution.py:442
  211.8 4.7 %collective-permute-done.26.refs_1_ = bf16[4,48,1536]{2,1,0:T(8,128)(2,1)S(1)} collective-permute-done((bf16[4,48,1536]{2,1,0:T(8,128)(2,1)S(1)}, bf16[4,48,1536]{2,1,0:T(8,128)(2,1)S(1)}, u32[]{:S(2)}, u32[]{:S(2)}) %collective-permute-start.26) | collective-permute-done | bytes 589856 | tf_op jit(solution)/shard_map/rs_ffn_2/ppermute | solution.py:49
  218.6 4.4 %rs_attn_deal_1.1 = (bf16[8,48,768]{2,1,0:T(8,128)(2,1)S(1)}, bf16[8,48,768]{2,1,0:T(8,128)(2,1)}, bf16[8,48,768]{2,1,0:T(8,128)(2,1)S(1)}, bf16[8,48,768]{2,1,0:T(8,128)(2,1)}) custom-call(bf16[1024,768]{1,0:T(8,128)(2,1)S(1)} %copy-done.2, bf16[1024,1152]{1,0:T(8,128)(2,1)S(1)} %get-tuple-element.213.refs_1_.x_ref, bf16[1024,768]{1,0:T(8,128)(2,1)S(1)} %copy-done.25, ...), custom_call_target="tpu_custom_call" | custom-call | flops 172500000 | bytes 1000 | tf_op jit(solution)/shard_map/rs_attn_deal_1/pallas_call | solution.py:237
  229.0 7.0 %all-to-all-start.3 = ((bf16[16,40,768]{2,1,0:T(8,128)(2,1)}), bf16[16,40,768]{2,1,0:T(8,128)(2,1)}, u32[]{:S(2)}, u32[]{:S(2)}) async-start(bf16[16,40,768]{2,1,0:T(8,128)(2,1)} %pad_maximum_fusion.2), calls=%async_computation.3 | async-start | bytes 1966080 | tf_op jit(solution)/shard_map/out_rows/all_to_all | solution.py:652
  250.6 6.6 %collective-permute-done.32.refs_1_ = bf16[4,48,768]{2,1,0:T(8,128)(2,1)S(1)} collective-permute-done((bf16[4,48,768]{2,1,0:T(8,128)(2,1)S(1)}, bf16[4,48,768]{2,1,0:T(8,128)(2,1)S(1)}, u32[]{:S(2)}, u32[]{:S(2)}) %collective-permute-start.32) | collective-permute-done | bytes 294944 | tf_op jit(solution)/shard_map/rs_attn_2/ppermute | solution.py:49
  261.0 5.7 %collective-permute-start.37 = (bf16[1,48,3072]{2,1,0:T(8,128)(2,1)S(1)}, bf16[1,48,3072]{2,1,0:T(8,128)(2,1)S(1)}, u32[]{:S(2)}, u32[]{:S(2)}) collective-permute-start(bf16[1,48,3072]{2,1,0:T(8,128)(2,1)S(1)} %get-tuple-element.240), channel_id=1, source_target_pairs={{0,16},{2,18},{4,20},{6,22},{8,24},{10,26},{12,28},{14,30},{16,0},... | collective-permute-start | bytes 884744 | tf_op jit(solution)/shard_map/rs_ffn_4/ppermute | solution.py:49
  267.3 6.1 %collective-permute-done.35.refs_1_ = bf16[2,48,1536]{2,1,0:T(8,128)(2,1)S(1)} collective-permute-done((bf16[2,48,1536]{2,1,0:T(8,128)(2,1)S(1)}, bf16[2,48,1536]{2,1,0:T(8,128)(2,1)S(1)}, u32[]{:S(2)}, u32[]{:S(2)}) %collective-permute-start.35) | collective-permute-done | bytes 294944 | tf_op jit(solution)/shard_map/rs_attn_3/ppermute | solution.py:49
  274.7 7.1 %collective-permute-done.37 = bf16[1,48,3072]{2,1,0:T(8,128)(2,1)S(1)} collective-permute-done((bf16[1,48,3072]{2,1,0:T(8,128)(2,1)S(1)}, bf16[1,48,3072]{2,1,0:T(8,128)(2,1)S(1)}, u32[]{:S(2)}, u32[]{:S(2)}) %collective-permute-start.37) | collective-permute-done | bytes 294944 | tf_op jit(solution)/shard_map/rs_ffn_4/ppermute | solution.py:49
  (269 shorter events, 126.8 us)
Async XLA Ops:
  7.2 112.5 %all-gather.2.cloned.1.call-start = ((), (), s32[]{:S(2)}) async-start(), calls=%async_computation.4 | async-start | bytes 2506752 | tf_op jit(solution)/shard_map/all_gather | solution.py:741
  8.5 14.5 %collective-permute-start.2 = (bf16[1,48,1152]{2,1,0:T(8,128)(2,1)S(1)}, bf16[1,48,1152]{2,1,0:T(8,128)(2,1)S(1)}, u32[]{:S(2)}, u32[]{:S(2)}) collective-permute-start(bf16[1,48,1152]{2,1,0:T(8,128)(2,1)S(1)} %broadcast_in_dim_reshape.3), channel_id=1, source_target_pairs={{0,24},{2,26},{4,28},{6,30},{8,16},{10,18},{12,20},{14,22},{16,8},... | collective-permute-start | bytes 331784 | tf_op jit(solution)/shard_map/ag_three_first/ppermute | solution.py:49
  22.9 26.6 %all-to-all-start = ((bf16[16,32,768]{2,1,0:T(8,128)(2,1)}), bf16[16,32,768]{2,1,0:T(8,128)(2,1)S(1)}, u32[]{:S(2)}, u32[]{:S(2)}) async-start(bf16[16,32,768]{2,1,0:T(8,128)(2,1)} %gather_fusion), calls=%async_computation | async-start | bytes 1572864 | tf_op jit(solution)/shard_map/in_tokens/all_to_all | solution.py:643
  44.1 13.7 %collective-permute-start.8 = (bf16[8,48,512]{2,1,0:T(8,128)(2,1)S(1)}, bf16[8,48,512]{2,1,0:T(8,128)(2,1)S(1)}, u32[]{:S(2)}, u32[]{:S(2)}) collective-permute-start(bf16[8,48,512]{2,1,0:T(8,128)(2,1)S(1)} %pad_maximum_fusion.7.refs_2_), channel_id=1, source_target_pairs={{0,4},{2,6},{4,0},{6,2},{8,12},{10,14},{12,8},{14,10},{16,20},{18,... | collective-permute-start | bytes 1179656 | tf_op jit(solution)/shard_map/ag_three_last/ppermute | solution.py:49
  47.0 15.6 %collective-permute-start.7 = (bf16[8,48,640]{2,1,0:T(8,128)(2,1)S(1)}, bf16[8,48,640]{2,1,0:T(8,128)(2,1)S(1)}, u32[]{:S(2)}, u32[]{:S(2)}) collective-permute-start(bf16[8,48,640]{2,1,0:T(8,128)(2,1)S(1)} %pad_maximum_fusion.6.refs_0_), channel_id=1, source_target_pairs={{0,2},{2,0},{4,6},{6,4},{8,10},{10,8},{12,14},{14,12},{16,18},{18,... | collective-permute-start | bytes 1474568 | tf_op jit(solution)/shard_map/ag_three_last/ppermute | solution.py:49
  49.6 14.7 %collective-permute-start.4 = (bf16[256,768]{1,0:T(8,128)(2,1)S(1)}, bf16[256,768]{1,0:T(8,128)(2,1)S(1)}, u32[]{:S(2)}, u32[]{:S(2)}) collective-permute-start(bf16[256,768]{1,0:T(8,128)(2,1)S(1)} %bitcast.93), channel_id=1, source_target_pairs={{0,1},{1,0},{2,3},{3,2},{4,5},{5,4},{6,7},{7,6},{8,9},{9,8},{10,11... | collective-permute-start | bytes 1179656 | tf_op jit(solution)/shard_map/ppermute | solution.py:49
  49.6 14.6 %collective-permute-start.3 = (bf16[256,768]{1,0:T(8,128)(2,1)S(1)}, bf16[256,768]{1,0:T(8,128)(2,1)S(1)}, u32[]{:S(2)}, u32[]{:S(2)}) collective-permute-start(bf16[256,768]{1,0:T(8,128)(2,1)S(1)} %bitcast.92), channel_id=1, source_target_pairs={{0,1},{1,0},{2,3},{3,2},{4,5},{5,4},{6,7},{7,6},{8,9},{9,8},{10,11... | collective-permute-start | bytes 1179656 | tf_op jit(solution)/shard_map/ppermute | solution.py:49
  50.2 22.5 %collective-permute-start.11 = (bf16[1,48,1920]{2,1,0:T(8,128)(2,1)}, bf16[1,48,1920]{2,1,0:T(8,128)(2,1)S(1)}, u32[]{:S(2)}, u32[]{:S(2)}) collective-permute-start(bf16[1,48,1920]{2,1,0:T(8,128)(2,1)} %bitcast.87), channel_id=1, source_target_pairs={{0,24},{2,26},{4,28},{6,30},{8,16},{10,18},{12,20},{14,22},{16,8},... | collective-permute-start | bytes 552968 | tf_op jit(solution)/shard_map/ag_rest_first/ppermute | solution.py:49
  57.8 17.0 %collective-permute-start.10 = (bf16[1,48,1920]{2,1,0:T(8,128)(2,1)}, bf16[1,48,1920]{2,1,0:T(8,128)(2,1)S(1)}, u32[]{:S(2)}, u32[]{:S(2)}) collective-permute-start(bf16[1,48,1920]{2,1,0:T(8,128)(2,1)} %bitcast.88), channel_id=1, source_target_pairs={{0,16},{2,18},{4,20},{6,22},{8,24},{10,26},{12,28},{14,30},{16,0},... | collective-permute-start | bytes 552968 | tf_op jit(solution)/shard_map/ag_rest_first/ppermute | solution.py:49
  74.9 17.8 %collective-permute-start.12 = (bf16[4,48,1024]{2,1,0:T(8,128)(2,1)S(1)}, bf16[4,48,1024]{2,1,0:T(8,128)(2,1)S(1)}, u32[]{:S(2)}, u32[]{:S(2)}) collective-permute-start(bf16[4,48,1024]{2,1,0:T(8,128)(2,1)S(1)} %slice.124), channel_id=1, source_target_pairs={{0,4},{2,6},{4,0},{6,2},{8,12},{10,14},{12,8},{14,10},{16,20},{18,... | collective-permute-start | bytes 1179656 | tf_op jit(solution)/shard_map/ag_rest_next/ppermute | solution.py:49
  77.2 14.5 %collective-permute-start.13 = (bf16[4,48,896]{2,1,0:T(8,128)(2,1)S(1)}, bf16[4,48,896]{2,1,0:T(8,128)(2,1)S(1)}, u32[]{:S(2)}, u32[]{:S(2)}) collective-permute-start(bf16[4,48,896]{2,1,0:T(8,128)(2,1)S(1)} %slice.125), channel_id=1, source_target_pairs={{0,2},{2,0},{4,6},{6,4},{8,10},{10,8},{12,14},{14,12},{16,18},{18,... | collective-permute-start | bytes 1032200 | tf_op jit(solution)/shard_map/ag_rest_next/ppermute | solution.py:49
  92.9 23.6 %collective-permute-start.14 = (bf16[8,48,1024]{2,1,0:T(8,128)(2,1)S(1)}, bf16[8,48,1024]{2,1,0:T(8,128)(2,1)}, u32[]{:S(2)}, u32[]{:S(2)}) collective-permute-start(bf16[8,48,1024]{2,1,0:T(8,128)(2,1)S(1)} %pad_maximum_fusion.3.refs_0_), channel_id=1, source_target_pairs={{0,2},{2,0},{4,6},{6,4},{8,10},{10,8},{12,14},{14,12},{16,18},{18,... | collective-permute-start | bytes 2359304 | tf_op jit(solution)/shard_map/ag_rest_last/ppermute | solution.py:49
  94.4 22.1 %collective-permute-start.15 = (bf16[8,48,896]{2,1,0:T(8,128)(2,1)S(1)}, bf16[8,48,896]{2,1,0:T(8,128)(2,1)S(1)}, u32[]{:S(2)}, u32[]{:S(2)}) collective-permute-start(bf16[8,48,896]{2,1,0:T(8,128)(2,1)S(1)} %pad_maximum_fusion.5.refs_2_), channel_id=1, source_target_pairs={{0,4},{2,6},{4,0},{6,2},{8,12},{10,14},{12,8},{14,10},{16,20},{18,... | collective-permute-start | bytes 2064392 | tf_op jit(solution)/shard_map/ag_rest_last/ppermute | solution.py:49
  99.2 37.8 %all-to-all-start.1 = ((bf16[16,32,768]{2,1,0:T(8,128)(2,1)}), bf16[16,32,768]{2,1,0:T(8,128)(2,1)}, u32[]{:S(2)}, u32[]{:S(2)}) async-start(bf16[16,32,768]{2,1,0:T(8,128)(2,1)} %gather_fusion.1), calls=%async_computation.1 | async-start | bytes 1572864 | tf_op jit(solution)/shard_map/in_cot/all_to_all | solution.py:643
  157.2 36.6 %collective-permute-start.24 = (bf16[8,48,1536]{2,1,0:T(8,128)(2,1)}, bf16[8,48,1536]{2,1,0:T(8,128)(2,1)}, u32[]{:S(2)}, u32[]{:S(2)}) collective-permute-start(bf16[8,48,1536]{2,1,0:T(8,128)(2,1)} %get-tuple-element.184), channel_id=1, source_target_pairs={{0,2},{2,0},{4,6},{6,4},{8,10},{10,8},{12,14},{14,12},{16,18},{18,... | collective-permute-start | bytes 3538952 | tf_op jit(solution)/shard_map/rs_ffn_10/ppermute | solution.py:49
  162.7 38.1 %collective-permute-start.25 = (bf16[8,48,1536]{2,1,0:T(8,128)(2,1)}, bf16[8,48,1536]{2,1,0:T(8,128)(2,1)}, u32[]{:S(2)}, u32[]{:S(2)}) collective-permute-start(bf16[8,48,1536]{2,1,0:T(8,128)(2,1)} %get-tuple-element.185), channel_id=1, source_target_pairs={{0,4},{2,6},{4,0},{6,2},{8,12},{10,14},{12,8},{14,10},{16,20},{18,... | collective-permute-start | bytes 3538952 | tf_op jit(solution)/shard_map/rs_ffn_11/ppermute | solution.py:49
  171.0 58.1 %all-to-all-start.2 = ((bf16[16,48,768]{2,1,0:T(8,128)(2,1)}), bf16[16,48,768]{2,1,0:T(8,128)(2,1)}, u32[]{:S(2)}, u32[]{:S(2)}) async-start(bf16[16,48,768]{2,1,0:T(8,128)(2,1)} %pad_maximum_fusion.1), calls=%async_computation.2 | async-start | bytes 2359296 | tf_op jit(solution)/shard_map/out_rows/all_to_all | solution.py:652
  204.2 13.3 %collective-permute-start.27 = (bf16[4,48,1536]{2,1,0:T(8,128)(2,1)S(1)}, bf16[4,48,1536]{2,1,0:T(8,128)(2,1)S(1)}, u32[]{:S(2)}, u32[]{:S(2)}) collective-permute-start(bf16[4,48,1536]{2,1,0:T(8,128)(2,1)S(1)} %get-tuple-element.200), channel_id=1, source_target_pairs={{0,2},{2,0},{4,6},{6,4},{8,10},{10,8},{12,14},{14,12},{16,18},{18,... | collective-permute-start | bytes 1769480 | tf_op jit(solution)/shard_map/rs_ffn_2/ppermute | solution.py:49
  225.9 16.4 %collective-permute-start.30 = (bf16[8,48,768]{2,1,0:T(8,128)(2,1)}, bf16[8,48,768]{2,1,0:T(8,128)(2,1)S(1)}, u32[]{:S(2)}, u32[]{:S(2)}) collective-permute-start(bf16[8,48,768]{2,1,0:T(8,128)(2,1)} %get-tuple-element.220), channel_id=1, source_target_pairs={{0,2},{2,0},{4,6},{6,4},{8,10},{10,8},{12,14},{14,12},{16,18},{18,... | collective-permute-start | bytes 1769480 | tf_op jit(solution)/shard_map/rs_attn_1/ppermute | solution.py:49
  226.5 19.1 %collective-permute-start.31 = (bf16[8,48,768]{2,1,0:T(8,128)(2,1)}, bf16[8,48,768]{2,1,0:T(8,128)(2,1)S(1)}, u32[]{:S(2)}, u32[]{:S(2)}) collective-permute-start(bf16[8,48,768]{2,1,0:T(8,128)(2,1)} %get-tuple-element.222), channel_id=1, source_target_pairs={{0,4},{2,6},{4,0},{6,2},{8,12},{10,14},{12,8},{14,10},{16,20},{18,... | collective-permute-start | bytes 1769480 | tf_op jit(solution)/shard_map/rs_attn_1/ppermute | solution.py:49
  227.4 23.1 %collective-permute-start.34 = (bf16[2,48,3072]{2,1,0:T(8,128)(2,1)}, bf16[2,48,3072]{2,1,0:T(8,128)(2,1)S(1)}, u32[]{:S(2)}, u32[]{:S(2)}) collective-permute-start(bf16[2,48,3072]{2,1,0:T(8,128)(2,1)} %get-tuple-element.230), channel_id=1, source_target_pairs={{0,8},{2,10},{4,12},{6,14},{8,0},{10,2},{12,4},{14,6},{16,24},{18,... | collective-permute-start | bytes 1769480 | tf_op jit(solution)/shard_map/rs_ffn_3/ppermute | solution.py:49
  229.0 53.8 %all-to-all-start.3 = ((bf16[16,40,768]{2,1,0:T(8,128)(2,1)}), bf16[16,40,768]{2,1,0:T(8,128)(2,1)}, u32[]{:S(2)}, u32[]{:S(2)}) async-start(bf16[16,40,768]{2,1,0:T(8,128)(2,1)} %pad_maximum_fusion.2), calls=%async_computation.3 | async-start | bytes 1966080 | tf_op jit(solution)/shard_map/out_rows/all_to_all | solution.py:652
  246.9 13.8 %collective-permute-start.33 = (bf16[4,48,768]{2,1,0:T(8,128)(2,1)S(1)}, bf16[4,48,768]{2,1,0:T(8,128)(2,1)S(1)}, u32[]{:S(2)}, u32[]{:S(2)}) collective-permute-start(bf16[4,48,768]{2,1,0:T(8,128)(2,1)S(1)} %get-tuple-element.226), channel_id=1, source_target_pairs={{0,2},{2,0},{4,6},{6,4},{8,10},{10,8},{12,14},{14,12},{16,18},{18,... | collective-permute-start | bytes 884744 | tf_op jit(solution)/shard_map/rs_attn_2/ppermute | solution.py:49
  261.0 20.9 %collective-permute-start.37 = (bf16[1,48,3072]{2,1,0:T(8,128)(2,1)S(1)}, bf16[1,48,3072]{2,1,0:T(8,128)(2,1)S(1)}, u32[]{:S(2)}, u32[]{:S(2)}) collective-permute-start(bf16[1,48,3072]{2,1,0:T(8,128)(2,1)S(1)} %get-tuple-element.240), channel_id=1, source_target_pairs={{0,16},{2,18},{4,20},{6,22},{8,24},{10,26},{12,28},{14,30},{16,0},... | collective-permute-start | bytes 884744 | tf_op jit(solution)/shard_map/rs_ffn_4/ppermute | solution.py:49
  (71 other events, 513.3 us)
Sparse Core Ops, SparseCore 0:
  14.4 85.5 all-gather.1
